TPU v7x, 128 devices: a whole 4x4x4 slice. The times are simulated.
128 devices in a mesh: dp: 4 (over z_lo, core), ctx: 32 (over z_hi, x, y).
Axes of the slice: x: 4, y: 4, z: 4 (z_hi: 2, z_lo: 2; z = z_hi * 2 + z_lo), core: 2. Of those that a mesh axis runs over, the one named last changes fastest.
Arguments:
- layer_input: bfloat16 [16384, 1024], P(('dp', 'ctx')), may hold values from -3 to 3
- query_heads: bfloat16 [16384, 512], P(('dp', 'ctx')), may hold values from -6 to 6
- key_heads: bfloat16 [16384, 512], P(('dp', 'ctx')), may hold values from -6 to 6
- value_heads: bfloat16 [16384, 512], P(('dp', 'ctx')), may hold values from -12 to 12
- out_weight: bfloat16 [1024, 512], replicated, may hold values from -0.25 to 0.25
- conv_kernel: bfloat16 [1024, 9], replicated, may hold values from -2 to 2
- record_lengths: int32 [4, 4], replicated, may hold values from 1 to 2048, 4096 in all within a row
- upstream_grad: bfloat16 [16384, 1024], P(('dp', 'ctx')), may hold values from -24 to 24
Outputs:
- layer_output: bfloat16 [16384, 1024], P(('dp', 'ctx'))
- input_grad: bfloat16 [16384, 1024], P(('dp', 'ctx'))
- query_grad: bfloat16 [16384, 512], P(('dp', 'ctx'))
- key_grad: bfloat16 [16384, 512], P(('dp', 'ctx'))
- value_grad: bfloat16 [16384, 512], P(('dp', 'ctx'))
- out_weight_grad: float32 [1024, 512], P(('dp', 'ctx'))
- kernel_grad: float32 [1024, 9], replicated
Inputs may be any that keep to these rules, and one draw needn't show every extreme that they name: `record_lengths`: each row lists the 4 recordings of one group in packing order; a row sums to 4096 and its longest recording has exactly 2048 frames.
All inputs are finite; a program needn't handle non-finite values.
Results may differ from a plain program's by a relative error of at most 0.023.
Values may be sent and summed in bfloat16 or wider, within the bound.
A program may use at most 128 MiB of HBM per device.

v0:
```python
import math

import jax
import jax.numpy as jnp
from jax import lax
from jax.sharding import PartitionSpec as P

H = 8
E = 64


SCORE_SCALE = 0.125
MASKED_SCORE = -1e30


def extended(shard, sides, width):
    for axis, dim in sides:
        count, length = (lax.axis_size(axis), shard.shape[dim])
        up = [(i, (i + 1) % count) for i in range(count - 1)]
        down = [(j, i) for i, j in up]
        last = lax.slice_in_dim(shard, length - width, length, axis=dim)
        leading = lax.slice_in_dim(shard, 0, width, axis=dim)
        before = lax.ppermute(last, axis, up)
        after = lax.ppermute(leading, axis, down)
        shard = jnp.concatenate([before, shard, after], axis=dim)
    return shard


def frame_ids(positions, record_sizes):
    record_ends = jnp.cumsum(record_sizes)
    record_starts = record_ends - record_sizes
    counted = jnp.sum((positions[:, None] >= record_starts[None, :]).astype(jnp.int32), axis=1)
    inside = (positions >= 0) & (positions < record_ends[-1])
    return jnp.where(inside, counted - 1, -1)


def block_ids(begin_row, row_total, record_sizes):
    return frame_ids(begin_row + jnp.arange(row_total, dtype=jnp.int32), record_sizes)


def heads_of(frames):
    return frames.reshape(frames.shape[0], H, E)


def masked_scores(query_split, key_rows, own_ids, other_ids):
    scores = (
        jnp.einsum(
            "qhe,khe->hqk", query_split, heads_of(key_rows), preferred_element_type=jnp.float32
        )
        * SCORE_SCALE
    )
    same_record = (own_ids[:, None] == other_ids[None, :])[None]
    return (jnp.where(same_record, scores, MASKED_SCORE), same_record)


def body(
    layer_input,
    query_heads,
    key_heads,
    value_heads,
    out_weight,
    conv_kernel,
    record_lengths,
    upstream_grad,
):
    row_count = layer_input.shape[0]
    feature_width = layer_input.shape[1]
    inner_width = query_heads.shape[1]
    tap_count = conv_kernel.shape[1]
    half_width = (tap_count - 1) // 2
    record_sizes = lax.dynamic_index_in_dim(record_lengths, lax.axis_index("dp"), 0, keepdims=False)
    first_frame = lax.axis_index("ctx") * row_count
    own_ids = block_ids(first_frame, row_count, record_sizes)
    query_split = heads_of(query_heads)
    group_span = lax.axis_size("ctx") * row_count
    block_rows = row_count * math.gcd(lax.axis_size("ctx"), max(1, -(-512 // row_count)))
    key_rows = lax.all_gather(key_heads, "ctx", axis=0, tiled=True)
    value_rows = lax.all_gather(value_heads, "ctx", axis=0, tiled=True)
    other_ids = block_ids(jnp.int32(0), key_rows.shape[0], record_sizes)
    running_max = jnp.full((H, row_count), MASKED_SCORE, jnp.float32)
    scores, same_record = masked_scores(query_split, key_rows, own_ids, other_ids)
    new_max = jnp.maximum(running_max, jnp.max(scores, axis=2))
    weights = jnp.where(same_record, jnp.exp(scores - new_max[:, :, None]), 0.0)
    new_sum = jnp.sum(weights, axis=2)
    update = jnp.einsum(
        "hqk,khe->hqe",
        weights,
        heads_of(value_rows).astype(jnp.float32),
        preferred_element_type=jnp.float32,
    )
    attended = (
        jnp.transpose(update / new_sum[:, :, None], (1, 0, 2))
        .reshape(row_count, inner_width)
        .astype(jnp.bfloat16)
    )
    log_norm = new_max + jnp.log(new_sum)
    mixed_frames = (
        layer_input.astype(jnp.float32)
        + lax.dot_general(
            attended, out_weight, (((1,), (1,)), ((), ())), preferred_element_type=jnp.float32
        )
    ).astype(jnp.bfloat16)
    padded = extended(mixed_frames, (("ctx", 0),), half_width)
    edge_ids = block_ids(first_frame - half_width, row_count + 2 * half_width, record_sizes)
    kernel_f32 = conv_kernel.astype(jnp.float32)

    def conv_tap(tap_index, running):
        shifted = lax.dynamic_slice_in_dim(padded, tap_index, row_count, 0).astype(jnp.float32)
        same_record = (lax.dynamic_slice_in_dim(edge_ids, tap_index, row_count, 0) == own_ids)[
            :, None
        ]
        tap_weight = lax.dynamic_slice_in_dim(kernel_f32, tap_index, 1, 1)[:, 0]
        return running + jnp.where(same_record, shifted * tap_weight[None, :], 0.0)

    conv_out = lax.fori_loop(
        0, tap_count, conv_tap, jnp.zeros((row_count, feature_width), jnp.float32)
    )
    sigmoid_gate = jax.nn.sigmoid(conv_out)
    layer_output = (mixed_frames.astype(jnp.float32) + conv_out * sigmoid_gate).astype(jnp.bfloat16)
    conv_grad = (
        upstream_grad.astype(jnp.float32) * sigmoid_gate * (1.0 + conv_out * (1.0 - sigmoid_gate))
    ).astype(jnp.bfloat16)
    grad_padded = extended(conv_grad, (("ctx", 0),), half_width)
    conv_grad_f32 = conv_grad.astype(jnp.float32)

    def back_tap(tap_index, carried):
        running, kernel_rows = carried
        mirror = tap_count - 1 - tap_index
        shifted = lax.dynamic_slice_in_dim(grad_padded, mirror, row_count, 0).astype(jnp.float32)
        same_back = (lax.dynamic_slice_in_dim(edge_ids, mirror, row_count, 0) == own_ids)[:, None]
        tap_weight = lax.dynamic_slice_in_dim(kernel_f32, tap_index, 1, 1)[:, 0]
        running = running + jnp.where(same_back, shifted * tap_weight[None, :], 0.0)
        forward_rows = lax.dynamic_slice_in_dim(padded, tap_index, row_count, 0).astype(jnp.float32)
        same_fore = (lax.dynamic_slice_in_dim(edge_ids, tap_index, row_count, 0) == own_ids)[
            :, None
        ]
        kernel_column = jnp.sum(jnp.where(same_fore, conv_grad_f32 * forward_rows, 0.0), axis=0)
        kernel_rows = lax.dynamic_update_slice_in_dim(
            kernel_rows, kernel_column[:, None], tap_index, 1
        )
        return (running, kernel_rows)

    back_sum, kernel_rows = lax.fori_loop(
        0,
        tap_count,
        back_tap,
        (
            jnp.zeros((row_count, feature_width), jnp.float32),
            jnp.zeros((feature_width, tap_count), jnp.float32),
        ),
    )
    input_grad = (upstream_grad.astype(jnp.float32) + back_sum).astype(jnp.bfloat16)
    kernel_grad = lax.psum(kernel_rows, ("dp", "ctx"))
    out_weight_grad = lax.psum_scatter(
        lax.dot_general(
            input_grad, attended, (((0,), (0,)), ((), ())), preferred_element_type=jnp.float32
        ),
        ("dp", "ctx"),
        scatter_dimension=0,
        tiled=True,
    )
    attended_grad = jnp.dot(input_grad, out_weight, preferred_element_type=jnp.float32).astype(
        jnp.bfloat16
    )
    grad_split = heads_of(attended_grad)
    row_dots = jnp.transpose(
        jnp.sum(grad_split.astype(jnp.float32) * heads_of(attended).astype(jnp.float32), axis=2)
    )
    gathered = (
        lax.all_gather(key_heads, "ctx", axis=0, tiled=True),
        lax.all_gather(value_heads, "ctx", axis=0, tiled=True),
    )

    def query_piece(carried, pieces, begin_row):
        key_rows, value_rows = pieces
        other_ids = block_ids(begin_row, key_rows.shape[0], record_sizes)
        scores, same_record = masked_scores(query_split, key_rows, own_ids, other_ids)
        probs = jnp.where(same_record, jnp.exp(scores - log_norm[:, :, None]), 0.0)
        grad_dots = jnp.einsum(
            "qhe,khe->hqk", grad_split, heads_of(value_rows), preferred_element_type=jnp.float32
        )
        score_grad = (probs * (grad_dots - row_dots[:, :, None])).astype(jnp.bfloat16)
        return carried + jnp.einsum(
            "hqk,khe->qhe", score_grad, heads_of(key_rows), preferred_element_type=jnp.float32
        )

    def run_block(block_index, carried):
        begin_row = block_index * block_rows
        pieces = (
            lax.dynamic_slice_in_dim(gathered[0], begin_row, block_rows, 0),
            lax.dynamic_slice_in_dim(gathered[1], begin_row, block_rows, 0),
        )
        return query_piece(carried, pieces, begin_row)

    query_sum = lax.fori_loop(
        0, group_span // block_rows, run_block, jnp.zeros((row_count, H, E), jnp.float32)
    )
    query_grad = (query_sum * SCORE_SCALE).reshape(row_count, inner_width).astype(jnp.bfloat16)
    key_rows = gathered[0]
    value_rows = gathered[1]
    other_ids = block_ids(jnp.int32(0), row_count * lax.axis_size("ctx"), record_sizes)
    scores, same_record = masked_scores(query_split, key_rows, own_ids, other_ids)
    probs = jnp.where(same_record, jnp.exp(scores - log_norm[:, :, None]), 0.0)
    grad_dots = jnp.einsum(
        "qhe,khe->hqk", grad_split, heads_of(value_rows), preferred_element_type=jnp.float32
    )
    score_grad = (probs * (grad_dots - row_dots[:, :, None])).astype(jnp.bfloat16)
    key_part = (
        jnp.einsum("hqk,qhe->khe", score_grad, query_split, preferred_element_type=jnp.float32)
        * SCORE_SCALE
    )
    value_part = jnp.einsum(
        "hqk,qhe->khe", probs.astype(jnp.bfloat16), grad_split, preferred_element_type=jnp.float32
    )
    key_value_sums = lax.psum_scatter(
        jnp.concatenate(
            [
                key_part.reshape(row_count * lax.axis_size("ctx"), inner_width),
                value_part.reshape(row_count * lax.axis_size("ctx"), inner_width),
            ],
            axis=1,
        ),
        "ctx",
        scatter_dimension=0,
        tiled=True,
    )
    key_grad = key_value_sums[:, :inner_width].astype(jnp.bfloat16)
    value_grad = key_value_sums[:, inner_width:].astype(jnp.bfloat16)
    return (
        layer_output,
        input_grad,
        query_grad,
        key_grad,
        value_grad,
        out_weight_grad,
        kernel_grad,
    )


def solution(mesh):
    placed = (
        P(("dp", "ctx"), None),
        P(("dp", "ctx"), None),
        P(("dp", "ctx"), None),
        P(("dp", "ctx"), None),
        P(),
        P(),
        P(),
        P(("dp", "ctx"), None),
    )
    return jax.shard_map(
        body,
        mesh=mesh,
        in_specs=placed,
        out_specs=(
            P(("dp", "ctx"), None),
            P(("dp", "ctx"), None),
            P(("dp", "ctx"), None),
            P(("dp", "ctx"), None),
            P(("dp", "ctx"), None),
            P(("dp", "ctx"), None),
            P(),
        ),
        check_vma=False,
    )
```

profile of v0, /device:TPU:96, one launch (start us, length us, event | category | flops | bytes accessed | tf_op | source)
XLA Modules:
  0.0 1300.0 jit_solution(12405632340498669019)
XLA Ops:
  17.1 91.0 %all-gather.3.cloned.1.call-done = bf16[4096,512]{0,1:T(8,128)(2,1)} async-done(((bf16[128,512]{0,1:T(8,128)(2,1)}), bf16[4096,512]{0,1:T(8,128)(2,1)}) %all-gather.3.cloned.1.call-update) | async-done | bytes 4194320 | tf_op jit(solution)/shard_map/all_gather | solution.py:77
  108.1 5.0 fusion.19
  113.7 5.1 copy-done.2
  118.8 5.4 fusion.16
  124.3 83.1 %all-gather.5.cloned.1.call-done = bf16[4096,512]{0,1:T(8,128)(2,1)} async-done(((bf16[128,512]{0,1:T(8,128)(2,1)}), bf16[4096,512]{0,1:T(8,128)(2,1)}) %all-gather.5.cloned.1.call-update) | async-done | bytes 4194320 | tf_op jit(solution)/shard_map/all_gather | solution.py:78
  207.4 11.3 fusion.35
  219.3 3.4 collective-permute-start
  222.7 8.2 collective-permute-start.1
  232.3 8.6 while.48
  246.1 10.1 collective-permute-start.3
  257.6 30.1 %while.49 = (s32[]{:T(128)}, f32[128,1024]{1,0:T(8,128)S(1)}, f32[1024,9]{0,1:T(8,128)}, s32[136]{0:T(256)}, s32[128]{0:T(128)}, /*index=5*/bf16[136,1024]{1,0:T...) while((s32[]{:T(128)}, f32[128,1024]{1,0:T(8,128)S(1)}, ...), condition=%wide.region_10.11_spmd.clone, body=%wide.region_8.10_spmd.clone.sunk | while | flops 1178887 | bytes 2123989 | solution.py:143
  290.2 10.6 fusion.20
  300.8 14.2 %convolution_multiply_fusion = f32[8,4096,64]{1,2,0:T(8,128)} fusion(bf16[128,8,64]{0,2,1:T(8,128)(2,1)S(1)} %bitcast.119, f32[8,128,4096]{2,1,0:T(8,128)} %copy-done.2, bf16[128,8,64]{0,2,1:T(8,128)(2,1)S(1)} %bitcast.127, bf16[4096,8,64]{0,2,1:T(8,128)(2,1)} %bitcast.122, f32[8,128]{1,0:T(8,128)S(1)} %bitcast.137, f32[8,128]{1,0:T(8,128)} %log_add_fusion, ...), kind=kOutput, calls=%fused_computation.52 | convolution fusion | flops 1105199104 | bytes 30154752 | tf_op jit(solution)/shard_map/hqk,qhe->khe/dot_general | solution.py:209
  315.0 9.0 copy.39
  324.1 9.0 copy.38
  333.1 11.7 pad_maximum_fusion
  347.6 69.2 %while.50 = (s32[]{:T(128)}, f32[128,8,64]{0,2,1:T(8,128)}, bf16[4096,512]{0,1:T(8,128)(2,1)}, s32[128]{0:T(128)S(1)}, s32[4,1]{0,1:T(1,128)}, /*index=5*/s32[1,...) while((s32[]{:T(128)}, f32[128,8,64]{0,2,1:T(8,128)}, ...), condition=%wide.region_14.15_spmd.clone, body=%wide.region_12.14_spmd.clone.sunk | while | flops 205202432 | bytes 10900241 | solution.py:195
  370.3 3.2 fusion.87
  379.0 3.1 fusion.87
  396.2 3.2 fusion.87
  404.9 3.2 fusion.87
  418.5 131.0 %psum.7 = f32[1024,9]{0,1:T(8,128)} all-reduce(f32[1024,9]{0,1:T(8,128)S(1)} %copy-done.15), channel_id=1, replica_groups=mesh['dp'=4,'ctx'=32] {'dp','ctx'}, use_global_device_ids=true, to_apply=%region_17.18 | all-reduce | flops 9216 | bytes 73728 | tf_op jit(solution)/shard_map/psum | solution.py:153
  549.5 23.1 %reduce-scatter.3.cloned.1.call-done = f32[128,1024]{1,0:T(8,128)} async-done(((f32[4096,1024]{1,0:T(8,128)}), f32[128,1024]{1,0:T(8,128)}) %reduce-scatter.3.cloned.1.call-update) | async-done | bytes 524304 | tf_op jit(solution)/shard_map/reduce_scatter | solution.py:215
  574.4 719.0 %reduce-scatter.5.cloned.1.call-done = f32[8,512]{1,0:T(8,128)} async-done(((f32[1024,512]{1,0:T(8,128)}), f32[8,512]{1,0:T(8,128)}) %reduce-scatter.5.cloned.1.call-update) | async-done | bytes 16400 | tf_op jit(solution)/shard_map/reduce_scatter | solution.py:154
  (231 shorter events, 122.2 us)
Async XLA Ops:
  7.2 211.6 %copy-start = (bf16[1024,512]{1,0:T(8,128)(2,1)S(1)}, bf16[1024,512]{1,0:T(8,128)(2,1)}, u32[]{:S(2)}) copy-start(bf16[1024,512]{1,0:T(8,128)(2,1)} %param.18) | copy-start | bytes 3145732
  7.2 100.9 %all-gather.3.cloned.1.call-start = ((), (), s32[]{:S(2)}) async-start(), calls=%async_computation.2 | async-start | bytes 4325376 | tf_op jit(solution)/shard_map/all_gather | solution.py:77
  9.0 198.4 %all-gather.5.cloned.1.call-start = ((), (), s32[]{:S(2)}) async-start(), calls=%async_computation.3 | async-start | bytes 4325376 | tf_op jit(solution)/shard_map/all_gather | solution.py:78
  10.7 561.9 %reduce-scatter.3.cloned.1.call-start = ((), (), s32[]{:S(2)}) async-start(), calls=%async_computation.4 | async-start | bytes 17301504 | tf_op jit(solution)/shard_map/reduce_scatter | solution.py:215
  15.1 0.9 copy-start.18
  113.1 5.7 copy-start.2
  124.2 94.5 %copy-start.20 = (f32[8,128]{1,0:T(8,128)}, f32[8,128]{1,0:T(8,128)S(1)}, u32[]{:S(2)}) copy-start(f32[8,128]{1,0:T(8,128)S(1)} %fusion.16) | copy-start | bytes 12292
  207.4 11.4 copy-start.10
  207.4 24.2 %copy-start.17 = (bf16[1024,9]{0,1:T(8,128)(2,1)S(1)}, bf16[1024,9]{0,1:T(8,128)(2,1)}, u32[]{:S(2)}) copy-start(bf16[1024,9]{0,1:T(8,128)(2,1)} %param.19) | copy-start | bytes 55300
  218.8 22.2 %copy-start.6 = (bf16[128,8,64]{0,2,1:T(8,128)(2,1)}, bf16[128,8,64]{0,2,1:T(8,128)(2,1)S(1)}, u32[]{:S(2)}) copy-start(bf16[128,8,64]{0,2,1:T(8,128)(2,1)S(1)} %fusion.35) | copy-start | bytes 393220
  219.3 21.7 %copy-start.4 = (bf16[128,1024]{1,0:T(8,128)(2,1)}, bf16[128,1024]{1,0:T(8,128)(2,1)S(1)}, u32[]{:S(2)}) copy-start(bf16[128,1024]{1,0:T(8,128)(2,1)S(1)} %fusion.32) | copy-start | bytes 786436
  219.3 12.3 collective-permute-start
  222.7 9.5 collective-permute-start.1
  244.2 13.3 %collective-permute-start.2 = (bf16[4,1024]{1,0:T(4,128)(2,1)S(1)}, bf16[4,1024]{1,0:T(4,128)(2,1)S(1)}, u32[]{:S(2)}, u32[]{:S(2)}) collective-permute-start(bf16[4,1024]{1,0:T(4,128)(2,1)S(1)} %get-tuple-element.776), channel_id=1, source_target_pairs={{0,1},{1,2},{2,3},{3,4},{4,5},{5,6},{6,7},{7,8},{8,9},{9,10},{10,1... | collective-permute-start | bytes 24584 | tf_op jit(solution)/shard_map/ppermute | solution.py:23
  246.1 11.4 collective-permute-start.3
  288.7 56.2 %copy-start.5 = (bf16[128,1024]{1,0:T(8,128)(2,1)}, bf16[128,1024]{1,0:T(8,128)(2,1)S(1)}, u32[]{:S(2)}) copy-start(bf16[128,1024]{1,0:T(8,128)(2,1)S(1)} %fusion.38) | copy-start | bytes 786436
  289.2 25.9 %copy-start.8 = (bf16[128,512]{0,1:T(8,128)(2,1)}, bf16[128,512]{0,1:T(8,128)(2,1)S(1)}, u32[]{:S(2)}) copy-start(bf16[128,512]{0,1:T(8,128)(2,1)S(1)} %copy.37) | copy-start | bytes 393220
  290.2 24.9 %copy-start.21 = (f32[128,8]{0,1:T(8,128)}, f32[128,8]{0,1:T(8,128)S(1)}, u32[]{:S(2)}) copy-start(f32[128,8]{0,1:T(8,128)S(1)} %multiply_reduce_fusion) | copy-start | bytes 12292
  344.8 2.7 copy-start.9
  344.8 2.7 copy-start.13
  344.8 2.7 copy-start.19
  344.8 948.6 %reduce-scatter.5.cloned.1.call-start = ((), (), s32[]{:S(2)}) async-start(), calls=%async_computation.5 | async-start | bytes 2113536 | tf_op jit(solution)/shard_map/reduce_scatter | solution.py:154
  347.5 945.9 %copy-start.1 = (bf16[1024,512]{1,0:T(8,128)(2,1)S(1)}, bf16[1024,512]{1,0:T(8,128)(2,1)}, u32[]{:S(2)}) copy-start(bf16[1024,512]{1,0:T(8,128)(2,1)} %param.18) | copy-start | bytes 3145732
  347.6 70.9 %copy-start.15 = (f32[1024,9]{0,1:T(8,128)S(1)}, f32[1024,9]{0,1:T(8,128)}, u32[]{:S(2)}) copy-start(f32[1024,9]{0,1:T(8,128)} %get-tuple-element.589) | copy-start | bytes 110596
  (13 other events, 9.9 us)
Sparse Core Ops, SparseCore 0:
  11.3 96.7 all-gather.2
  111.4 95.9 all-gather.4
  345.0 227.5 reduce-scatter.2
  575.4 718.0 reduce-scatter.4
where the time goes:
time: 1300 us
  waiting for transfers between devices  917 us (71%)
  blocking collectives  131 us (10%)
  local copies, waits for them, and re-layouts  86.1 us (7%)
  matrix products  72.9 us (6%)
  other arithmetic  54.6 us (4%)
  starting transfers between devices  23.7 us (2%)
  between operations  14.2 us (1%)
    reduce_scatter x1, waiting for transfers between devices, body(): lax.psum_scatter(lax.dot_general(input_grad, attended, (((0,), (0,)), (()...  719 us
    psum x1, blocking collectives, body(): kernel_grad = lax.psum(kernel_rows, ('dp', 'ctx'))  131 us
    all_gather x1, waiting for transfers between devices, body(): key_rows = lax.all_gather(key_heads, 'ctx', axis=0, tiled=True)  91 us
    all_gather x1, waiting for transfers between devices, body(): value_rows = lax.all_gather(value_heads, 'ctx', axis=0, tiled=True)  83.1 us
  transfers between devices with their start and end apart: 8, of which 5 were waited for; matrix products, arithmetic and copies ran while one was open for 7% of the time, Pallas kernels for 0%

commit v1 on v0

v1 whole, which is shorter than its diff:
```python
import functools

import jax
import jax.numpy as jnp
from jax import lax
from jax.experimental import pallas as pl
from jax.experimental.pallas import tpu as pltpu
from jax.sharding import PartitionSpec as P

MESH = pl.DeviceIdType.MESH
BF = jnp.bfloat16
F32 = jnp.float32
H = 8
E = 64
SCALE = 0.125
NEG = -1e30
T = 128
KB = 256
NB = 4096 // KB


def vm(n):
    return [pl.BlockSpec(memory_space=pltpu.VMEM)] * n


def params(cid):
    return pltpu.CompilerParams(collective_id=cid, has_side_effects=True)


def meet_plane(me):
    barrier = pltpu.get_barrier_semaphore()

    def hello(d, _):
        pl.semaphore_signal(barrier, inc=1, device_id={"ctx": (me + 4 * d) % 32}, device_id_type=MESH)
        return 0

    lax.fori_loop(1, 8, hello, 0)
    pl.semaphore_wait(barrier, 7)


def meet_group(me):
    barrier = pltpu.get_barrier_semaphore()

    def hello(d, _):
        pl.semaphore_signal(barrier, inc=1, device_id={"ctx": (me + d) % 32}, device_id_type=MESH)
        return 0

    lax.fori_loop(1, 32, hello, 0)
    pl.semaphore_wait(barrier, 31)


def plane_copy(me, d, src, dst, send_sem, recv_sem):
    other = (me + 4 * d) % 32
    return pltpu.make_async_remote_copy(
        src_ref=src.at[other // 4],
        dst_ref=dst.at[me // 4],
        send_sem=send_sem.at[d],
        recv_sem=recv_sem.at[d],
        device_id={"ctx": other},
        device_id_type=MESH,
    )


def group_copy(me, d, src, dst, send_sem, recv_sem, by_head):
    other = (me + d) % 32
    return pltpu.make_async_remote_copy(
        src_ref=src.at[other // 4] if by_head else src.at[other],
        dst_ref=dst.at[me],
        send_sem=send_sem.at[d],
        recv_sem=recv_sem.at[d],
        device_id={"ctx": other},
        device_id_type=MESH,
    )


def gather_kernel(q_ref, k_ref, v_ref, kv_out, q_out, kvs, qs, ks, kr, qsnd, qrcv, own):
    me = lax.axis_index("ctx")
    for h in range(H):
        cols = slice(h * E, (h + 1) * E)
        kvs[h] = jnp.concatenate([k_ref[:, cols], v_ref[:, cols]], axis=1)
    qt = (q_ref[...].astype(F32) * SCALE).T.astype(BF)
    for h in range(H):
        qs[h] = qt[h * E : (h + 1) * E, :]
    meet_group(me)

    def start(d, _):
        group_copy(me, d, kvs, kv_out, ks, kr, True).start()
        return 0

    def start_q(d, _):
        plane_copy(me, d, qs, q_out, qsnd, qrcv).start()
        return 0

    lax.fori_loop(1, 8, start_q, 0)
    lax.fori_loop(1, 32, start, 0)
    a = pltpu.make_async_copy(kvs.at[me // 4], kv_out.at[me], own.at[0])
    b = pltpu.make_async_copy(qs.at[me // 4], q_out.at[me // 4], own.at[1])
    a.start()
    b.start()
    a.wait()
    b.wait()

    def done(d, _):
        group_copy(me, d, kvs, kv_out, ks, kr, True).wait()
        return 0

    def done_q(d, _):
        plane_copy(me, d, qs, q_out, qsnd, qrcv).wait()
        return 0

    lax.fori_loop(1, 8, done_q, 0)
    lax.fori_loop(1, 32, done, 0)


def gather_qkv(q, k, v):
    return pl.pallas_call(
        gather_kernel,
        name="gather_qkv",
        out_shape=(
            jax.ShapeDtypeStruct((32, T, 2 * E), BF),
            jax.ShapeDtypeStruct((H, E, T), BF),
        ),
        in_specs=vm(3),
        out_specs=tuple(vm(2)),
        scratch_shapes=[
            pltpu.VMEM((H, T, 2 * E), BF),
            pltpu.VMEM((H, E, T), BF),
            pltpu.SemaphoreType.DMA((32,)),
            pltpu.SemaphoreType.DMA((32,)),
            pltpu.SemaphoreType.DMA((8,)),
            pltpu.SemaphoreType.DMA((8,)),
            pltpu.SemaphoreType.DMA((2,)),
        ],
        compiler_params=params(0),
    )(q, k, v)


def plane_kernel(x_ref, y_ref, snd, rcv, own):
    me = lax.axis_index("ctx")
    meet_plane(me)

    def start(d, _):
        plane_copy(me, d, x_ref, y_ref, snd, rcv).start()
        return 0

    lax.fori_loop(1, 8, start, 0)
    a = pltpu.make_async_copy(x_ref.at[me // 4], y_ref.at[me // 4], own)
    a.start()
    a.wait()

    def done(d, _):
        plane_copy(me, d, x_ref, y_ref, snd, rcv).wait()
        return 0

    lax.fori_loop(1, 8, done, 0)


def plane_exchange(x, cid, name):
    return pl.pallas_call(
        plane_kernel,
        name=name,
        out_shape=jax.ShapeDtypeStruct(x.shape, x.dtype),
        in_specs=vm(1),
        out_specs=vm(1)[0],
        scratch_shapes=[
            pltpu.SemaphoreType.DMA((8,)),
            pltpu.SemaphoreType.DMA((8,)),
            pltpu.SemaphoreType.DMA,
        ],
        compiler_params=params(cid),
    )(x)


def spread_kernel(dq_ref, dkv_ref, dq_out, dkv_out, ks, kr, qsnd, qrcv, own):
    me = lax.axis_index("ctx")
    meet_group(me)

    def start(d, _):
        group_copy(me, d, dkv_ref, dkv_out, ks, kr, False).start()
        return 0

    def start_q(d, _):
        plane_copy(me, d, dq_ref, dq_out, qsnd, qrcv).start()
        return 0

    lax.fori_loop(1, 32, start, 0)
    lax.fori_loop(1, 8, start_q, 0)
    a = pltpu.make_async_copy(dkv_ref.at[me], dkv_out.at[me], own.at[0])
    b = pltpu.make_async_copy(dq_ref.at[me // 4], dq_out.at[me // 4], own.at[1])
    a.start()
    b.start()
    a.wait()
    b.wait()

    def done(d, _):
        group_copy(me, d, dkv_ref, dkv_out, ks, kr, False).wait()
        return 0

    def done_q(d, _):
        plane_copy(me, d, dq_ref, dq_out, qsnd, qrcv).wait()
        return 0

    lax.fori_loop(1, 8, done_q, 0)
    lax.fori_loop(1, 32, done, 0)


def finish_kernel(dq_ref, dkv_ref, dq_out, dk_out, dv_out):
    dq = (dq_ref[...].astype(F32).reshape(H * E, T) * SCALE).T
    dq_out[...] = dq.astype(BF)
    for h in range(H):
        total = dkv_ref[4 * h].astype(F32)
        for p in range(1, 4):
            total = total + dkv_ref[4 * h + p].astype(F32)
        cols = slice(h * E, (h + 1) * E)
        dk_out[:, cols] = total[:, :E].astype(BF)
        dv_out[:, cols] = total[:, E:].astype(BF)


def spread_grads(dq, dkv):
    dq_all, dkv_all = pl.pallas_call(
        spread_kernel,
        name="spread_grads",
        out_shape=(
            jax.ShapeDtypeStruct((H, E, T), BF),
            jax.ShapeDtypeStruct((32, T, 2 * E), BF),
        ),
        in_specs=vm(2),
        out_specs=tuple(vm(2)),
        scratch_shapes=[
            pltpu.SemaphoreType.DMA((32,)),
            pltpu.SemaphoreType.DMA((32,)),
            pltpu.SemaphoreType.DMA((8,)),
            pltpu.SemaphoreType.DMA((8,)),
            pltpu.SemaphoreType.DMA((2,)),
        ],
        compiler_params=params(3),
    )(dq, dkv)
    return pl.pallas_call(
        finish_kernel,
        name="finish_grads",
        out_shape=(jax.ShapeDtypeStruct((T, H * E), BF),) * 3,
        in_specs=vm(2),
        out_specs=tuple(vm(3)),
    )(dq_all, dkv_all)


def record_bounds(len_ref):
    g = lax.axis_index("dp")
    s1 = len_ref[g, 0]
    s2 = s1 + len_ref[g, 1]
    s3 = s2 + len_ref[g, 2]
    return s1, s2, s3, s3 + len_ref[g, 3]


def low_of(pos, b):
    return jnp.where(pos >= b[2], b[2], jnp.where(pos >= b[1], b[1], jnp.where(pos >= b[0], b[0], 0)))


def high_of(pos, b):
    return jnp.where(pos < b[0], b[0], jnp.where(pos < b[1], b[1], jnp.where(pos < b[2], b[2], b[3])))


def block_span(i, part, b):
    f0 = (i * 4 + part) * T
    pos = f0 + lax.broadcasted_iota(jnp.int32, (1, T), 1)
    lo, hi = low_of(pos, b), high_of(pos, b)
    first_lo, first_hi = low_of(f0, b), high_of(f0, b)
    last_hi = high_of(f0 + T - 1, b)
    kb0 = first_lo // KB
    kb1 = (last_hi + KB - 1) // KB
    same = first_hi == last_hi
    in0 = jnp.where(same, (first_lo + KB - 1) // KB, kb1)
    in1 = jnp.where(same, first_hi // KB, kb1)
    in0 = jnp.minimum(in0, kb1)
    in1 = jnp.maximum(in1, in0)
    return lo, hi, kb0, in0, in1, kb1


def fold(x, op):
    r = x.reshape(x.shape[0] // 8, 8, x.shape[1])
    return op(r, axis=0)


def forward_kernel(len_ref, kv_ref, q_ref, att_ref, lse_ref, kvt_ref, st):
    part = lax.axis_index("ctx") % 4
    b = record_bounds(len_ref)

    def turn(j, _):
        kvt_ref[j] = kv_ref[j].astype(F32).T.astype(BF)
        return 0

    lax.fori_loop(0, NB, turn, 0)

    def block(i, _):
        lo, hi, kb0, in0, in1, kb1 = block_span(i, part, b)
        qz = jnp.concatenate([q_ref[i], jnp.zeros((E, T), BF)], axis=0)

        def score(masked):
            def step(j, m):
                s = jnp.dot(kv_ref[j], qz, preferred_element_type=F32)
                if masked:
                    kpos = j * KB + lax.broadcasted_iota(jnp.int32, (KB, T), 0)
                    s = jnp.where((kpos >= lo) & (kpos < hi), s, NEG)
                st[j] = s
                return jnp.maximum(m, fold(s, jnp.max))

            return step

        m = jnp.full((8, T), NEG, F32)
        m = lax.fori_loop(kb0, in0, score(True), m)
        m = lax.fori_loop(in0, in1, score(False), m)
        m = lax.fori_loop(in1, kb1, score(True), m)
        m = jnp.max(m, axis=0, keepdims=True)

        def weigh(j, carry):
            l, acc = carry
            p = jnp.exp(st[j] - m)
            l = l + fold(p, jnp.sum)
            acc = acc + jnp.dot(kvt_ref[j], p.astype(BF), preferred_element_type=F32)
            return l, acc

        l, acc = lax.fori_loop(kb0, kb1, weigh, (jnp.zeros((8, T), F32), jnp.zeros((2 * E, T), F32)))
        l = jnp.sum(l, axis=0, keepdims=True)
        att_ref[i] = (acc[E:] / l).astype(BF)
        lse_ref[i] = m + jnp.log(l)
        return 0

    lax.fori_loop(0, H, block, 0)


def forward(lens, kv, q):
    return pl.pallas_call(
        forward_kernel,
        name="attention_forward",
        out_shape=(
            jax.ShapeDtypeStruct((H, E, T), BF),
            jax.ShapeDtypeStruct((H, 1, T), F32),
            jax.ShapeDtypeStruct((NB, 2 * E, KB), BF),
        ),
        in_specs=[pl.BlockSpec(memory_space=pltpu.SMEM)] + vm(2),
        out_specs=tuple(vm(3)),
        scratch_shapes=[pltpu.VMEM((NB, KB, T), F32)],
    )(lens, kv.reshape(NB, KB, 2 * E), q)


def backward_kernel(len_ref, kv_ref, kvt_ref, q_ref, do_ref, att_ref, lse_ref, dq_ref, dkv_ref, acc_ref):
    part = lax.axis_index("ctx") % 4
    b = record_bounds(len_ref)

    def clear(j, _):
        acc_ref[j] = jnp.zeros((KB, 2 * E), F32)
        return 0

    lax.fori_loop(0, NB, clear, 0)

    def block(i, _):
        lo, hi, kb0, in0, in1, kb1 = block_span(i, part, b)
        qt, dot = q_ref[i], do_ref[i]
        rows = jnp.sum(dot.astype(F32) * att_ref[i].astype(F32), axis=0, keepdims=True)
        lse = lse_ref[i]
        zero = jnp.zeros((E, T), BF)
        both = jnp.concatenate(
            [jnp.concatenate([qt, zero], axis=0), jnp.concatenate([zero, dot], axis=0)], axis=1
        )
        back = both.astype(F32).T.astype(BF)

        def step(masked):
            def body(j, dq):
                sd = jnp.dot(kv_ref[j], both, preferred_element_type=F32)
                p = jnp.exp(sd[:, :T] - lse)
                if masked:
                    kpos = j * KB + lax.broadcasted_iota(jnp.int32, (KB, T), 0)
                    p = jnp.where((kpos >= lo) & (kpos < hi), p, 0.0)
                ds = (p * (sd[:, T:] - rows)).astype(BF)
                dq = dq + jnp.dot(kvt_ref[j], ds, preferred_element_type=F32)
                acc_ref[j] += jnp.dot(
                    jnp.concatenate([ds, p.astype(BF)], axis=1), back, preferred_element_type=F32
                )
                return dq

            return body

        dq = jnp.zeros((2 * E, T), F32)
        dq = lax.fori_loop(kb0, in0, step(True), dq)
        dq = lax.fori_loop(in0, in1, step(False), dq)
        dq = lax.fori_loop(in1, kb1, step(True), dq)
        dq_ref[i] = dq[:E].astype(BF)
        return 0

    lax.fori_loop(0, H, block, 0)

    def put(j, _):
        dkv_ref[j] = acc_ref[j].astype(BF)
        return 0

    lax.fori_loop(0, NB, put, 0)


def backward(lens, kv, kvt, q, do, att, lse):
    dq, dkv = pl.pallas_call(
        backward_kernel,
        name="attention_backward",
        out_shape=(
            jax.ShapeDtypeStruct((H, E, T), BF),
            jax.ShapeDtypeStruct((NB, KB, 2 * E), BF),
        ),
        in_specs=[pl.BlockSpec(memory_space=pltpu.SMEM)] + vm(6),
        out_specs=tuple(vm(2)),
        scratch_shapes=[pltpu.VMEM((NB, KB, 2 * E), F32)],
    )(lens, kv.reshape(NB, KB, 2 * E), kvt, q, do, att, lse)
    return dq, dkv.reshape(32, T, 2 * E)


def everyone(me, d):
    other = (me + d) % 128
    return other, {"dp": other // 32, "ctx": other % 32}


def weight_kernel(w_ref, o_ref, ws, got, snd, rcv):
    me = lax.axis_index("dp") * 32 + lax.axis_index("ctx")
    barrier = pltpu.get_barrier_semaphore()

    def hello(d, _):
        _, where = everyone(me, d)
        pl.semaphore_signal(barrier, inc=1, device_id=where, device_id_type=MESH)
        return 0

    lax.fori_loop(1, 128, hello, 0)
    ws[...] = w_ref[...].astype(BF)
    pl.semaphore_wait(barrier, 127)

    def copy(d):
        other, where = everyone(me, d)
        return pltpu.make_async_remote_copy(
            src_ref=ws.at[other],
            dst_ref=got.at[d],
            send_sem=snd.at[d],
            recv_sem=rcv.at[d],
            device_id=where,
            device_id_type=MESH,
        )

    def start(d, _):
        copy(d).start()
        return 0

    lax.fori_loop(1, 128, start, 0)
    total = w_ref[me]

    def done(d, total):
        copy(d).wait()
        return total + got[d].astype(F32)

    o_ref[...] = lax.fori_loop(1, 128, done, total)


def weight_scatter(w):
    return pl.pallas_call(
        weight_kernel,
        name="weight_scatter",
        out_shape=jax.ShapeDtypeStruct((8, 512), F32),
        in_specs=vm(1),
        out_specs=vm(1)[0],
        scratch_shapes=[
            pltpu.VMEM((128, 8, 512), BF),
            pltpu.VMEM((128, 8, 512), BF),
            pltpu.SemaphoreType.DMA((128,)),
            pltpu.SemaphoreType.DMA((128,)),
        ],
        compiler_params=params(4),
    )(w.reshape(128, 8, 512))


def with_sides(x, width):
    n = 32
    up = [(i, i + 1) for i in range(n - 1)]
    down = [(j, i) for i, j in up]
    before = lax.ppermute(x[-width:], "ctx", up)
    after = lax.ppermute(x[:width], "ctx", down)
    return jnp.concatenate([before, x, after], axis=0)


def frame_ids(positions, sizes):
    ends = jnp.cumsum(sizes)
    counted = jnp.sum((positions[:, None] >= (ends - sizes)[None, :]).astype(jnp.int32), axis=1)
    inside = (positions >= 0) & (positions < ends[-1])
    return jnp.where(inside, counted - 1, -1)


def body(x, q, k, v, w, ck, lens, g):
    n, taps, half = T, 9, 4
    kv, qs = gather_qkv(q, k, v)
    att_t, lse, kvt = forward(lens, kv, qs)
    att_own = plane_exchange(att_t, 1, "attended_home")
    attended = att_own.reshape(H * E, T).T
    mixed = (
        x.astype(F32)
        + lax.dot_general(attended, w, (((1,), (1,)), ((), ())), preferred_element_type=F32)
    ).astype(BF)
    sizes = lax.dynamic_index_in_dim(lens, lax.axis_index("dp"), 0, keepdims=False)
    first = lax.axis_index("ctx") * n
    ids = frame_ids(first - half + jnp.arange(n + 2 * half, dtype=jnp.int32), sizes)
    own = ids[half : half + n]
    padded = with_sides(mixed, half).astype(F32)
    kf = ck.astype(F32).T
    conv = jnp.zeros((n, 1024), F32)
    for j in range(taps):
        same = (ids[j : j + n] == own)[:, None]
        conv = conv + jnp.where(same, padded[j : j + n] * kf[j][None], 0.0)
    gate = jax.nn.sigmoid(conv)
    layer_output = (mixed.astype(F32) + conv * gate).astype(BF)
    cg = (g.astype(F32) * gate * (1.0 + conv * (1.0 - gate))).astype(BF)
    cgf = cg.astype(F32)
    gp = with_sides(cg, half).astype(F32)
    back = jnp.zeros((n, 1024), F32)
    rows = []
    for j in range(taps):
        mirror = taps - 1 - j
        same = (ids[mirror : mirror + n] == own)[:, None]
        back = back + jnp.where(same, gp[mirror : mirror + n] * kf[j][None], 0.0)
        fore = (ids[j : j + n] == own)[:, None]
        rows.append(jnp.sum(jnp.where(fore, cgf * padded[j : j + n], 0.0), axis=0))
    input_grad = (g.astype(F32) + back).astype(BF)
    kernel_grad = lax.psum(jnp.stack(rows), ("dp", "ctx")).T
    wg = lax.dot_general(
        input_grad, attended, (((0,), (0,)), ((), ())), preferred_element_type=F32
    )
    ag_t = lax.dot_general(w, input_grad, (((0,), (1,)), ((), ())), preferred_element_type=F32).astype(BF)
    do = plane_exchange(ag_t.reshape(H, E, T), 2, "grad_out")
    dq, dkv = backward(lens, kv, kvt, qs, do, att_t, lse)
    dq, dk, dv = spread_grads(dq, dkv)
    return layer_output, input_grad, dq, dk, dv, weight_scatter(wg), kernel_grad


def solution(mesh):
    row = P(("dp", "ctx"), None)
    return jax.shard_map(
        body,
        mesh=mesh,
        in_specs=(row, row, row, row, P(), P(), P(), row),
        out_specs=(row, row, row, row, row, row, P()),
        check_vma=False,
    )
```

time: 1300 us -> 244 us (0.19)
  the two profiles are of different devices: /device:TPU:96 before, /device:TPU:1 now
where the time goes in v1:
time: 244 us
  Pallas kernels  140 us (57%)
  blocking collectives  79.6 us (33%)
  starting transfers between devices  11.4 us (5%)
  other arithmetic  5.71 us (2%)
  matrix products  3.6 us (1%)
    psum x1, blocking collectives, body(): kernel_grad = lax.psum(jnp.stack(rows), ('dp', 'ctx')).T  79.6 us
    pallas_call x1, Pallas kernels, weight_scatter(): pl.pallas_call(weight_kernel, name='weight_scatter', out_shape=jax.ShapeD...  27.4 us
    pallas_call x1, Pallas kernels, gather_qkv(): pl.pallas_call(gather_kernel, name='gather_qkv', out_shape=(jax.ShapeDtyp...  26.8 us
    pallas_call x1, Pallas kernels, spread_grads(): pl.pallas_call(spread_kernel, name='spread_grads', out_shape=(jax.ShapeDt...  23.9 us
    pallas_call x1, Pallas kernels, backward(): pl.pallas_call(backward_kernel, name='attention_backward', out_shape=(jax...  23.1 us
    pallas_call x1, Pallas kernels, forward(): pl.pallas_call(forward_kernel, name='attention_forward', out_shape=(jax.S...  19.2 us
    pallas_call x2, Pallas kernels, plane_exchange(): pl.pallas_call(plane_kernel, name=name, out_shape=jax.ShapeDtypeStruct(x....  17.4 us
    ppermute x2, starting transfers between devices, with_sides(): before = lax.ppermute(x[-width:], 'ctx', up)  8.77 us
  transfers between devices with their start and end apart: 4, of which 0 were waited for; matrix products, arithmetic and copies ran while one was open for 1% of the time, Pallas kernels for 0%

profile of v1, /device:TPU:1, one launch (start us, length us, event | category | flops | bytes accessed | tf_op | source)
XLA Modules:
  0.0 243.6 jit_solution(541411235963874954)
XLA Ops:
  0.7 26.8 %gather_qkv.1 = (bf16[32,128,128]{2,1,0:T(8,128)(2,1)}, bf16[8,64,128]{2,1,0:T(8,128)(2,1)}) custom-call(bf16[128,512]{1,0:T(8,128)(2,1)} %q_ref.1, bf16[128,512]{1,0:T(8,128)(2,1)} %k_ref.1, bf16[128,512]{1,0:T(8,128)(2,1)} %v_ref.1), custom_call_target="tpu_custom_call" | custom-call | tf_op jit(solution)/shard_map/gather_qkv/pallas_call | solution.py:116
  27.5 19.2 %attention_forward.1 = (bf16[8,64,128]{2,1,0:T(8,128)(2,1)}, f32[8,1,128]{2,1,0:T(1,128)}, bf16[16,128,256]{2,1,0:T(8,128)(2,1)}) custom-call(s32[4,4]{1,0:T(4,128)} %len_ref.3, bf16[16,256,128]{2,1,0:T(8,128)(2,1)} %bitcast.47, bf16[8,64,128]{2,1,0:T(8,128)(2,1)} %get-tuple-element.20.q_ref), custom_call_target="tpu_custom_call" | custom-call | tf_op jit(solution)/shard_map/attention_forward/pallas_call | solution.py:332
  46.6 9.1 %attended_home.1 = bf16[8,64,128]{2,1,0:T(8,128)(2,1)} custom-call(bf16[8,64,128]{2,1,0:T(8,128)(2,1)} %get-tuple-element.21.x_ref.att_ref), custom_call_target="tpu_custom_call" | custom-call | tf_op jit(solution)/shard_map/attended_home/pallas_call | solution.py:159
  55.7 1.5 fusion
  57.3 1.3 collective-permute-start.1
  58.6 4.0 %collective-permute-start = (bf16[4,1024]{1,0:T(4,128)(2,1)S(1)}, bf16[4,1024]{1,0:T(4,128)(2,1)S(1)}, u32[]{:S(2)}, u32[]{:S(2)}) collective-permute-start(bf16[4,1024]{1,0:T(4,128)(2,1)S(1)} %get-tuple-element.44), channel_id=1, source_target_pairs={{0,1},{1,2},{2,3},{3,4},{4,5},{5,6},{6,7},{7,8},{8,9},{9,10},{10,1... | collective-permute-start | bytes 24584 | tf_op jit(solution)/shard_map/ppermute | solution.py:478
  62.6 0.2 reduce-window.4
  62.8 0.6 slice.161
  63.5 0.7 and_select_fusion
  64.3 2.8 %fusion.21 = (f32[1024]{0:T(1024)S(1)}, f32[1024]{0:T(1024)S(1)}, f32[1024]{0:T(1024)S(1)}, f32[1024]{0:T(1024)S(1)}, f32[1024]{0:T(1024)S(1)}, /*index=5*/f32[1...) fusion(f32[136,1024]{1,0:T(8,128)S(1)} %maximum_convert_fusion,, ...), kind=kLoop, calls=%fused_computation.34 | loop fusion | flops 8117248 | bytes 5841920 | tf_op jit(solution)/shard_map/reduce_sum | solution.py:522
  67.2 0.9 add_convert_fusion
  68.1 1.3 collective-permute-start.3
  69.4 4.8 %collective-permute-start.2 = (bf16[4,1024]{1,0:T(4,128)(2,1)S(1)}, bf16[4,1024]{1,0:T(4,128)(2,1)S(1)}, u32[]{:S(2)}, u32[]{:S(2)}) collective-permute-start(bf16[4,1024]{1,0:T(4,128)(2,1)S(1)} %get-tuple-element.42), channel_id=1, source_target_pairs={{0,1},{1,2},{2,3},{3,4},{4,5},{5,6},{6,7},{7,8},{8,9},{9,10},{10,1... | collective-permute-start | bytes 24584 | tf_op jit(solution)/shard_map/ppermute | solution.py:478
  74.2 79.6 %psum.7 = f32[1024,9]{0,1:T(8,128)} all-reduce(f32[1024,9]{0,1:T(8,128)S(1)} %bitcast.54), channel_id=1, replica_groups=mesh['dp'=4,'ctx'=32] {'dp','ctx'}, use_global_device_ids=true, to_apply=%region_11.12 | all-reduce | flops 9216 | bytes 73728 | tf_op jit(solution)/shard_map/psum | solution.py:524
  153.9 0.9 fusion.4
  154.8 0.3 fusion.1
  155.1 0.8 copy.22
  155.9 8.4 %grad_out.1.do_ref = bf16[8,64,128]{2,1,0:T(8,128)(2,1)} custom-call(bf16[8,64,128]{2,1,0:T(8,128)(2,1)} %bitcast.53), custom_call_target="tpu_custom_call" | custom-call | tf_op jit(solution)/shard_map/grad_out/pallas_call | solution.py:159
  164.5 1.8 fusion.38.w_ref
  166.3 27.4 %weight_scatter.1 = f32[8,512]{1,0:T(8,128)} custom-call(f32[128,8,512]{2,1,0:T(8,128)} %fusion.38.w_ref), custom_call_target="tpu_custom_call" | custom-call | tf_op jit(solution)/shard_map/weight_scatter/pallas_call | solution.py:458
  193.7 23.1 %attention_backward.1 = (bf16[8,64,128]{2,1,0:T(8,128)(2,1)}, bf16[16,256,128]{2,1,0:T(8,128)(2,1)}) custom-call(s32[4,4]{1,0:T(4,128)} %len_ref.3, bf16[16,256,128]{2,1,0:T(8,128)(2,1)} %bitcast.48, bf16[16,128,256]{2,1,0:T(8,128)(2,1)} %get-tuple-element.22.kvt_ref, bf16[8,64,128]{2,1,0:T(8,128)(2,1)} %get-tuple-element.20.q_ref, ...), custom_call_target="tpu_custom_call" | custom-call | tf_op jit(solution)/shard_map/attention_backward/pallas_call | solution.py:400
  216.8 23.9 %spread_grads.1 = (bf16[8,64,128]{2,1,0:T(8,128)(2,1)}, bf16[32,128,128]{2,1,0:T(8,128)(2,1)}) custom-call(bf16[8,64,128]{2,1,0:T(8,128)(2,1)} %get-tuple-element.24.dq_ref, bf16[32,128,128]{2,1,0:T(8,128)(2,1)} %bitcast.52), custom_call_target="tpu_custom_call" | custom-call | tf_op jit(solution)/shard_map/spread_grads/pallas_call | solution.py:220
  240.7 2.3 finish_grads.1
  243.0 0.6 copy.29
  (31 shorter events, 0.7 us)
Async XLA Ops:
  0.6 55.1 %copy-start = (bf16[1024,512]{1,0:T(8,128)(2,1)S(1)}, bf16[1024,512]{1,0:T(8,128)(2,1)}, u32[]{:S(2)}) copy-start(bf16[1024,512]{1,0:T(8,128)(2,1)} %param.12) | copy-start | bytes 3145732
  0.6 61.9 %copy-start.6 = (s32[4,4]{1,0:T(4,128)S(1)}, s32[4,4]{1,0:T(4,128)}, u32[]{:S(2)}) copy-start(s32[4,4]{1,0:T(4,128)} %len_ref.3) | copy-start | bytes 196
  0.7 62.7 %copy-start.5 = (bf16[1024,9]{0,1:T(8,128)(2,1)S(1)}, bf16[1024,9]{0,1:T(8,128)(2,1)}, u32[]{:S(2)}) copy-start(bf16[1024,9]{0,1:T(8,128)(2,1)} %param.13) | copy-start | bytes 55300
  27.5 36.9 %copy-start.3 = (bf16[128,1024]{1,0:T(8,128)(2,1)S(1)}, bf16[128,1024]{1,0:T(8,128)(2,1)}, u32[]{:S(2)}) copy-start(bf16[128,1024]{1,0:T(8,128)(2,1)} %param.15) | copy-start | bytes 786436
  57.3 7.0 %collective-permute-start.1 = (bf16[4,1024]{1,0:T(4,128)(2,1)S(1)}, bf16[4,1024]{1,0:T(4,128)(2,1)S(1)}, u32[]{:S(2)}, u32[]{:S(2)}) collective-permute-start(bf16[4,1024]{1,0:T(4,128)(2,1)S(1)} %get-tuple-element.45), channel_id=1, source_target_pairs={{1,0},{2,1},{3,2},{4,3},{5,4},{6,5},{7,6},{8,7},{9,8},{10,9},{11,1... | collective-permute-start | bytes 24584 | tf_op jit(solution)/shard_map/ppermute | solution.py:479
  58.6 5.7 %collective-permute-start = (bf16[4,1024]{1,0:T(4,128)(2,1)S(1)}, bf16[4,1024]{1,0:T(4,128)(2,1)S(1)}, u32[]{:S(2)}, u32[]{:S(2)}) collective-permute-start(bf16[4,1024]{1,0:T(4,128)(2,1)S(1)} %get-tuple-element.44), channel_id=1, source_target_pairs={{0,1},{1,2},{2,3},{3,4},{4,5},{5,6},{6,7},{7,8},{8,9},{9,10},{10,1... | collective-permute-start | bytes 24584 | tf_op jit(solution)/shard_map/ppermute | solution.py:478
  68.1 85.8 %collective-permute-start.3 = (bf16[4,1024]{1,0:T(4,128)(2,1)S(1)}, bf16[4,1024]{1,0:T(4,128)(2,1)S(1)}, u32[]{:S(2)}, u32[]{:S(2)}) collective-permute-start(bf16[4,1024]{1,0:T(4,128)(2,1)S(1)} %get-tuple-element.43), channel_id=1, source_target_pairs={{1,0},{2,1},{3,2},{4,3},{5,4},{6,5},{7,6},{8,7},{9,8},{10,9},{11,1... | collective-permute-start | bytes 24584 | tf_op jit(solution)/shard_map/ppermute | solution.py:479
  69.4 84.5 %collective-permute-start.2 = (bf16[4,1024]{1,0:T(4,128)(2,1)S(1)}, bf16[4,1024]{1,0:T(4,128)(2,1)S(1)}, u32[]{:S(2)}, u32[]{:S(2)}) collective-permute-start(bf16[4,1024]{1,0:T(4,128)(2,1)S(1)} %get-tuple-element.42), channel_id=1, source_target_pairs={{0,1},{1,2},{2,3},{3,4},{4,5},{5,6},{6,7},{7,8},{8,9},{9,10},{10,1... | collective-permute-start | bytes 24584 | tf_op jit(solution)/shard_map/ppermute | solution.py:478
  154.8 11.5 %copy-start.1 = (bf16[128,1024]{1,0:T(8,128)(2,1)}, bf16[128,1024]{1,0:T(8,128)(2,1)S(1)}, u32[]{:S(2)}) copy-start(bf16[128,1024]{1,0:T(8,128)(2,1)S(1)} %fusion.4) | copy-start | bytes 786436
  154.8 9.7 %copy-start.2 = (bf16[8,64,128]{2,1,0:T(8,128)(2,1)S(1)}, bf16[8,64,128]{2,1,0:T(8,128)(2,1)}, u32[]{:S(2)}) copy-start(bf16[8,64,128]{2,1,0:T(8,128)(2,1)} %attended_home.1) | copy-start | bytes 393220
  193.7 49.3 %copy-start.4 = (f32[8,512]{1,0:T(8,128)S(1)}, f32[8,512]{1,0:T(8,128)}, u32[]{:S(2)}) copy-start(f32[8,512]{1,0:T(8,128)} %weight_scatter.1) | copy-start | bytes 49156

commit v2 on v1

v2 whole, which is shorter than its diff:
```python
import functools

import jax
import jax.numpy as jnp
from jax import lax
from jax.experimental import pallas as pl
from jax.experimental.pallas import tpu as pltpu
from jax.sharding import PartitionSpec as P

MESH = pl.DeviceIdType.MESH
BF = jnp.bfloat16
F32 = jnp.float32
H = 8
E = 64
SCALE = 0.125
NEG = -1e30
T = 128
KB = 256
NB = 4096 // KB


def vm(n):
    return [pl.BlockSpec(memory_space=pltpu.VMEM)] * n


def params(cid):
    return pltpu.CompilerParams(collective_id=cid, has_side_effects=True)


def barrier_hello(me):
    barrier = pltpu.get_barrier_semaphore()

    def hello(d, _):
        pl.semaphore_signal(barrier, inc=1, device_id={"ctx": (me + d) % 32}, device_id_type=MESH)
        return 0

    lax.fori_loop(1, 32, hello, 0)


def barrier_wait():
    pl.semaphore_wait(pltpu.get_barrier_semaphore(), 31)


def plane_copy(me, d, src, dst, send_sem, recv_sem):
    other = (me + 4 * d) % 32
    return pltpu.make_async_remote_copy(
        src_ref=src.at[other // 4],
        dst_ref=dst.at[me // 4],
        send_sem=send_sem.at[d],
        recv_sem=recv_sem.at[d],
        device_id={"ctx": other},
        device_id_type=MESH,
    )


def group_copy(me, d, src, dst, send_sem, recv_sem, by_head):
    other = (me + d) % 32
    return pltpu.make_async_remote_copy(
        src_ref=src.at[other // 4] if by_head else src.at[other],
        dst_ref=dst.at[me],
        send_sem=send_sem.at[d],
        recv_sem=recv_sem.at[d],
        device_id={"ctx": other},
        device_id_type=MESH,
    )


def gather_kernel(q_ref, k_ref, v_ref, x_ref, g_ref, kv_out, q_out, halo, kvs, qs, ks, kr, qsnd, qrcv, own, hsnd, hrcv):
    me = lax.axis_index("ctx")
    barrier_hello(me)
    for h in range(H):
        cols = slice(h * E, (h + 1) * E)
        kvs[h] = jnp.concatenate([k_ref[:, cols], v_ref[:, cols]], axis=1)
    qt = (q_ref[...].astype(F32) * SCALE).T.astype(BF)
    for h in range(H):
        qs[h] = qt[h * E : (h + 1) * E, :]
    barrier_wait()

    def start(d, _):
        group_copy(me, d, kvs, kv_out, ks, kr, True).start()
        return 0

    def start_q(d, _):
        plane_copy(me, d, qs, q_out, qsnd, qrcv).start()
        return 0

    def side(a, up):
        ref = (x_ref, g_ref)[a]
        return pltpu.make_async_remote_copy(
            src_ref=ref.at[pl.ds(T - 8, 8)] if up else ref.at[pl.ds(0, 8)],
            dst_ref=halo.at[a, 0 if up else 1],
            send_sem=hsnd.at[a, 0 if up else 1],
            recv_sem=hrcv.at[a, 0 if up else 1],
            device_id={"ctx": (me + (1 if up else 31)) % 32},
            device_id_type=MESH,
        )

    lax.fori_loop(1, 8, start_q, 0)
    lax.fori_loop(1, 32, start, 0)
    sides = [side(a, up) for a in range(2) for up in (True, False)]
    for c in sides:
        c.start()
    a = pltpu.make_async_copy(kvs.at[me // 4], kv_out.at[me], own.at[0])
    b = pltpu.make_async_copy(qs.at[me // 4], q_out.at[me // 4], own.at[1])
    a.start()
    b.start()
    a.wait()
    b.wait()

    def done(d, _):
        group_copy(me, d, kvs, kv_out, ks, kr, True).wait()
        return 0

    def done_q(d, _):
        plane_copy(me, d, qs, q_out, qsnd, qrcv).wait()
        return 0

    lax.fori_loop(1, 8, done_q, 0)
    lax.fori_loop(1, 32, done, 0)
    for c in sides:
        c.wait()


def gather_qkv(q, k, v, x, g):
    return pl.pallas_call(
        gather_kernel,
        name="gather_qkv",
        out_shape=(
            jax.ShapeDtypeStruct((32, T, 2 * E), BF),
            jax.ShapeDtypeStruct((H, E, T), BF),
            jax.ShapeDtypeStruct((2, 2, 8, 1024), BF),
        ),
        in_specs=vm(5),
        out_specs=tuple(vm(3)),
        scratch_shapes=[
            pltpu.VMEM((H, T, 2 * E), BF),
            pltpu.VMEM((H, E, T), BF),
            pltpu.SemaphoreType.DMA((32,)),
            pltpu.SemaphoreType.DMA((32,)),
            pltpu.SemaphoreType.DMA((8,)),
            pltpu.SemaphoreType.DMA((8,)),
            pltpu.SemaphoreType.DMA((2,)),
            pltpu.SemaphoreType.DMA((2, 2)),
            pltpu.SemaphoreType.DMA((2, 2)),
        ],
        compiler_params=params(0),
    )(q, k, v, x, g)


def mid_kernel(
    len_ref, att_ref, edge_ref, x_ref, g_ref, halo, w_ref, ck_ref,
    lo_ref, ig_ref, do_ref, wg_ref, kg_ref,
    at_in, eb, am, ap, igs, igp, dos, mx, ge, cs, mk,
    asnd, arcv, esnd, ercv, dsnd, drcv, psnd, prcv, own,
):
    dp, me = lax.axis_index("dp"), lax.axis_index("ctx")
    core, part, plane = dp % 2, me % 4, me // 4
    partner = {"dp": dp - core + (1 - core)}
    barrier = pltpu.get_barrier_semaphore()

    def signal(where):
        pl.semaphore_signal(barrier, inc=1, device_id=where, device_id_type=MESH)

    signal(partner)

    def hello(d, _):
        signal({"ctx": (me + 4 * d) % 32})
        return 0

    def hello_edge(i, _):
        signal({"ctx": (4 * i + part + 1) % 32})
        signal({"ctx": (4 * i + part + 31) % 32})
        return 0

    lax.fori_loop(1, 8, hello, 0)
    lax.fori_loop(0, 8, hello_edge, 0)

    s1, s2, s3, s4 = record_bounds(len_ref)

    def label(pos):
        one = lambda s: jnp.where(pos >= s, 1, 0)
        n = one(s1) + one(s2) + one(s3)
        return jnp.where((pos >= 0) & (pos < s4), n, -1)

    pos = me * T - 4 + lax.broadcasted_iota(jnp.int32, (136, 128), 0)
    mine = label(pos)
    for j in range(9):
        mk[j] = jnp.where(label(pos + (j - 4)) == mine, 1.0, 0.0)
    ge[0:8] = halo[1, 0].astype(F32)
    ge[8:136] = g_ref[...].astype(F32)
    ge[136:144] = halo[1, 1].astype(F32)

    pl.semaphore_wait(barrier, 24)

    def att_copy(d):
        return plane_copy(me, d, att_ref, at_in, asnd, arcv)

    def edge_copy(i, late):
        other = (4 * i + part + (1 if late else 31)) % 32
        return pltpu.make_async_remote_copy(
            src_ref=edge_ref.at[i, 1 if late else 0],
            dst_ref=eb.at[0 if late else 1, plane],
            send_sem=esnd.at[1 if late else 0, i],
            recv_sem=ercv.at[0 if late else 1, plane],
            device_id={"ctx": other},
            device_id_type=MESH,
        )

    def edge_arrival(h, side):
        return pltpu.make_async_remote_copy(
            src_ref=edge_ref.at[0, 0],
            dst_ref=eb.at[side, h],
            send_sem=esnd.at[0, 0],
            recv_sem=ercv.at[side, h],
            device_id=partner,
            device_id_type=MESH,
        )

    def start_att(d, _):
        att_copy(d).start()
        return 0

    def start_edge(i, _):
        edge_copy(i, True).start()
        edge_copy(i, False).start()
        return 0

    lax.fori_loop(1, 8, start_att, 0)
    lax.fori_loop(0, 8, start_edge, 0)
    a = pltpu.make_async_copy(att_ref.at[plane], at_in.at[plane], own.at[0])
    a.start()
    a.wait()

    def wait_att(d, _):
        att_copy(d).wait()
        return 0

    def wait_edge(i, _):
        edge_copy(i, True).wait_send()
        edge_copy(i, False).wait_send()
        edge_arrival(i, 0).wait_recv()
        edge_arrival(i, 1).wait_recv()
        return 0

    lax.fori_loop(1, 8, wait_att, 0)
    lax.fori_loop(0, 8, wait_edge, 0)
    am[...] = at_in[...].astype(F32).reshape(H * E, T).T.astype(BF)

    def pair(src, dst, n):
        return pltpu.make_async_remote_copy(
            src_ref=src,
            dst_ref=dst,
            send_sem=psnd.at[n],
            recv_sem=prcv.at[n],
            device_id=partner,
            device_id_type=MESH,
        )

    send_att = pair(am, ap, 0)
    send_att.start()
    sides = jnp.concatenate(
        [jnp.concatenate([eb[s, h][:, :E] for h in range(H)], axis=1) for s in range(2)], axis=0
    )

    NT = (((1,), (1,)), ((), ()))

    def chunk(c, _):
        cols = pl.ds(pl.multiple_of(c * 128, 128), 128)
        wc = w_ref[cols, :]
        main = lax.dot_general(am[...], wc, NT, preferred_element_type=F32)
        rim = lax.dot_general(sides, wc, NT, preferred_element_type=F32)
        rnd = lambda y: y.astype(BF).astype(F32)
        mx[8:136] = rnd(x_ref[:, cols].astype(F32) + main)
        mx[0:8] = rnd(halo[0, 0, :, cols].astype(F32) + rim[0:8])
        mx[136:144] = rnd(halo[0, 1, :, cols].astype(F32) + rim[8:16])
        conv = jnp.zeros((136, 128), F32)
        for j in range(9):
            conv = conv + mx[pl.ds(j, 136)] * mk[j] * ck_ref[j : j + 1, cols]
        gate = jax.nn.sigmoid(conv)
        cg = ge[pl.ds(4, 136), cols] * gate * (1.0 + conv * (1.0 - gate))
        cs[...] = rnd(cg)
        silu = conv * gate
        lo_ref[:, cols] = (mx[8:136] + silu[4:132]).astype(BF)
        back = ge[8:136, cols]
        for j in range(9):
            back = back + cs[pl.ds(8 - j, 128)] * mk[8 - j, pl.ds(4, 128)] * ck_ref[j : j + 1, cols]
        ig = back.astype(BF)
        ig_ref[:, cols] = ig
        igs[c // 2, :, pl.ds(pl.multiple_of((c % 2) * 128, 128), 128)] = ig
        cg_own = cs[pl.ds(4, 128)]
        rows = []
        for j in range(9):
            rows.append(
                jnp.sum(cg_own * mx[pl.ds(4 + j, 128)] * mk[j, pl.ds(4, 128)], axis=0, keepdims=True)
            )
        rows.append(jnp.zeros((7, 128), F32))
        kg_ref[c] = jnp.concatenate(rows, axis=0)
        return 0

    lax.fori_loop(0, 8, chunk, 0)
    send_ig = [pair(igs.at[2 * z + 1 - core], igp.at[z], 1 + z) for z in range(2)]
    for c in send_ig:
        c.start()
    ag = jnp.zeros((T, H * E), F32)
    for z in range(4):
        ag = ag + jnp.dot(igs[z], w_ref[z * 256 : (z + 1) * 256, :], preferred_element_type=F32)
    dos[...] = ag.astype(BF).astype(F32).T.astype(BF).reshape(H, E, T)

    def do_copy(d):
        return plane_copy(me, d, dos, do_ref, dsnd, drcv)

    def start_do(d, _):
        do_copy(d).start()
        return 0

    lax.fori_loop(1, 8, start_do, 0)
    b = pltpu.make_async_copy(dos.at[plane], do_ref.at[plane], own.at[1])
    b.start()
    send_att.wait()
    for c in send_ig:
        c.wait()
    TN = (((0,), (0,)), ((), ()))
    for z in range(2):
        wg = lax.dot_general(igs[2 * z + core], am[...], TN, preferred_element_type=F32)
        wg = wg + lax.dot_general(igp[z], ap[...], TN, preferred_element_type=F32)
        wg_ref[z * 32 : (z + 1) * 32] = wg.reshape(32, 8, H * E).astype(BF)
    b.wait()

    def wait_do(d, _):
        do_copy(d).wait()
        return 0

    lax.fori_loop(1, 8, wait_do, 0)


def middle(lens, att, edge, x, g, halo, w, ck):
    sem = pltpu.SemaphoreType.DMA
    return pl.pallas_call(
        mid_kernel,
        name="middle",
        out_shape=(
            jax.ShapeDtypeStruct((T, 1024), BF),
            jax.ShapeDtypeStruct((T, 1024), BF),
            jax.ShapeDtypeStruct((H, E, T), BF),
            jax.ShapeDtypeStruct((64, 8, H * E), BF),
            jax.ShapeDtypeStruct((8, 16, 128), F32),
        ),
        in_specs=[pl.BlockSpec(memory_space=pltpu.SMEM)] + vm(7),
        out_specs=tuple(vm(5)),
        scratch_shapes=[
            pltpu.VMEM((H, E, T), BF),
            pltpu.VMEM((2, H, 8, 128), BF),
            pltpu.VMEM((T, H * E), BF),
            pltpu.VMEM((T, H * E), BF),
            pltpu.VMEM((4, T, 256), BF),
            pltpu.VMEM((2, T, 256), BF),
            pltpu.VMEM((H, E, T), BF),
            pltpu.VMEM((144, 128), F32),
            pltpu.VMEM((144, 1024), F32),
            pltpu.VMEM((136, 128), F32),
            pltpu.VMEM((9, 136, 128), F32),
            sem((8,)),
            sem((8,)),
            sem((2, 8)),
            sem((2, 8)),
            sem((8,)),
            sem((8,)),
            sem((3,)),
            sem((3,)),
            sem((2,)),
        ],
        compiler_params=params(1),
    )(lens, att, edge, x, g, halo, w, ck)


def spread_kernel(
    dq_ref, dkv_ref, wg_ref, kg_ref, dq_out, dk_out, dv_out, wo_ref, ko_ref,
    dq_in, dkv_in, wg_in, k1, k2, ksum, kall,
    ks, kr, qsnd, qrcv, wsnd, wrcv, s1, r1, s2, r2, s3, r3, own,
):
    dp, me = lax.axis_index("dp"), lax.axis_index("ctx")
    core, part, plane = dp % 2, me % 4, me // 4
    chip = (dp // 2) * 32 + me
    barrier = pltpu.get_barrier_semaphore()

    def chip_at(d):
        other = (chip + d) % 64
        return other, {"dp": (other // 32) * 2 + core, "ctx": other % 32}

    def column_at(d):
        other = (dp * 4 + part + d) % 16
        return {"dp": other // 4, "ctx": plane * 4 + other % 4}

    def hello(d, _):
        pl.semaphore_signal(barrier, inc=1, device_id=chip_at(d)[1], device_id_type=MESH)
        return 0

    def hello_column(d, _):
        where = {"dp": (d // 4) * 2 + 1 - core, "ctx": plane * 4 + d % 4}
        pl.semaphore_signal(barrier, inc=1, device_id=where, device_id_type=MESH)
        return 0

    lax.fori_loop(1, 64, hello, 0)
    lax.fori_loop(0, 8, hello_column, 0)
    pl.semaphore_wait(barrier, 71)

    def loop(n, f):
        def step(d, _):
            f(d)
            return 0

        lax.fori_loop(1, n, step, 0)

    def w_copy(d):
        other, where = chip_at(d)
        return pltpu.make_async_remote_copy(
            src_ref=wg_ref.at[other],
            dst_ref=wg_in.at[d],
            send_sem=wsnd.at[d],
            recv_sem=wrcv.at[d],
            device_id=where,
            device_id_type=MESH,
        )

    def column_copy(d):
        return pltpu.make_async_remote_copy(
            src_ref=ksum.at[0],
            dst_ref=k2.at[dp * 4 + part],
            send_sem=s2.at[d],
            recv_sem=r2.at[d],
            device_id=column_at(d),
            device_id_type=MESH,
        )

    def back_copy(d):
        return pltpu.make_async_remote_copy(
            src_ref=ksum.at[1],
            dst_ref=kall.at[plane],
            send_sem=s3.at[d],
            recv_sem=r3.at[d],
            device_id={"ctx": (me + 4 * d) % 32},
            device_id_type=MESH,
        )

    rows = lambda d: plane_copy(me, d, kg_ref, k1, s1, r1)
    grads = lambda d: group_copy(me, d, dkv_ref, dkv_in, ks, kr, False)
    queries = lambda d: plane_copy(me, d, dq_ref, dq_in, qsnd, qrcv)
    loop(8, lambda d: rows(d).start())
    loop(32, lambda d: grads(d).start())
    loop(8, lambda d: queries(d).start())
    loop(64, lambda d: w_copy(d).start())
    a = pltpu.make_async_copy(dkv_ref.at[me], dkv_in.at[me], own.at[0])
    b = pltpu.make_async_copy(dq_ref.at[plane], dq_in.at[plane], own.at[1])
    c = pltpu.make_async_copy(kg_ref.at[plane], k1.at[plane], own.at[2])
    for copy in (a, b, c):
        copy.start()
    for copy in (a, b, c):
        copy.wait()
    loop(8, lambda d: rows(d).wait())
    ksum[0] = jnp.sum(k1[...], axis=0)
    k2[dp * 4 + part] = ksum[0]
    loop(16, lambda d: column_copy(d).start())
    loop(16, lambda d: column_copy(d).wait())
    ksum[1] = jnp.sum(k2[...], axis=0)
    kall[plane] = ksum[1]
    loop(8, lambda d: back_copy(d).start())
    loop(8, lambda d: queries(d).wait())
    dq_out[...] = (dq_in[...].astype(F32).reshape(H * E, T) * SCALE).T.astype(BF)
    loop(32, lambda d: grads(d).wait())
    for h in range(H):
        total = dkv_in[4 * h].astype(F32)
        for p in range(1, 4):
            total = total + dkv_in[4 * h + p].astype(F32)
        cols = slice(h * E, (h + 1) * E)
        dk_out[:, cols] = total[:, :E].astype(BF)
        dv_out[:, cols] = total[:, E:].astype(BF)

    def add(d, total):
        w_copy(d).wait()
        return total + wg_in[d].astype(F32)

    wo_ref[...] = lax.fori_loop(1, 64, add, wg_ref[chip].astype(F32))
    loop(8, lambda d: back_copy(d).wait())
    ko_ref[...] = kall[...]


def spread_grads(dq, dkv, wg, kg):
    sem = pltpu.SemaphoreType.DMA
    return pl.pallas_call(
        spread_kernel,
        name="spread_grads",
        out_shape=(jax.ShapeDtypeStruct((T, H * E), BF),) * 3
        + (jax.ShapeDtypeStruct((8, H * E), F32), jax.ShapeDtypeStruct((8, 16, 128), F32)),
        in_specs=vm(4),
        out_specs=tuple(vm(5)),
        scratch_shapes=[
            pltpu.VMEM((H, E, T), BF),
            pltpu.VMEM((32, T, 2 * E), BF),
            pltpu.VMEM((64, 8, H * E), BF),
            pltpu.VMEM((8, 16, 128), F32),
            pltpu.VMEM((16, 16, 128), F32),
            pltpu.VMEM((2, 16, 128), F32),
            pltpu.VMEM((8, 16, 128), F32),
            sem((32,)),
            sem((32,)),
            sem((8,)),
            sem((8,)),
            sem((64,)),
            sem((64,)),
            sem((8,)),
            sem((8,)),
            sem((16,)),
            sem((16,)),
            sem((8,)),
            sem((8,)),
            sem((3,)),
        ],
        compiler_params=params(2),
    )(dq, dkv, wg, kg)


def record_bounds(len_ref):
    g = lax.axis_index("dp")
    s1 = len_ref[g, 0]
    s2 = s1 + len_ref[g, 1]
    s3 = s2 + len_ref[g, 2]
    return s1, s2, s3, s3 + len_ref[g, 3]


def low_of(pos, b):
    return jnp.where(pos >= b[2], b[2], jnp.where(pos >= b[1], b[1], jnp.where(pos >= b[0], b[0], 0)))


def high_of(pos, b):
    return jnp.where(pos < b[0], b[0], jnp.where(pos < b[1], b[1], jnp.where(pos < b[2], b[2], b[3])))


def block_span(i, part, b):
    f0 = (i * 4 + part) * T
    pos = f0 + lax.broadcasted_iota(jnp.int32, (1, T), 1)
    lo, hi = low_of(pos, b), high_of(pos, b)
    first_lo, first_hi = low_of(f0, b), high_of(f0, b)
    last_hi = high_of(f0 + T - 1, b)
    kb0 = first_lo // KB
    kb1 = (last_hi + KB - 1) // KB
    same = first_hi == last_hi
    in0 = jnp.where(same, (first_lo + KB - 1) // KB, kb1)
    in1 = jnp.where(same, first_hi // KB, kb1)
    in0 = jnp.minimum(in0, kb1)
    in1 = jnp.maximum(in1, in0)
    return lo, hi, kb0, in0, in1, kb1


def fold(x, op):
    r = x.reshape(x.shape[0] // 8, 8, x.shape[1])
    return op(r, axis=0)


def forward_kernel(len_ref, kv_ref, q_ref, att_ref, edge_ref, lse_ref, kvt_ref, st):
    part = lax.axis_index("ctx") % 4
    b = record_bounds(len_ref)

    def turn(j, _):
        kvt_ref[j] = kv_ref[j].astype(F32).T.astype(BF)
        return 0

    lax.fori_loop(0, NB, turn, 0)

    def block(i, _):
        lo, hi, kb0, in0, in1, kb1 = block_span(i, part, b)
        qz = jnp.concatenate([q_ref[i], jnp.zeros((E, T), BF)], axis=0)

        def score(masked):
            def step(j, m):
                s = jnp.dot(kv_ref[j], qz, preferred_element_type=F32)
                if masked:
                    kpos = j * KB + lax.broadcasted_iota(jnp.int32, (KB, T), 0)
                    s = jnp.where((kpos >= lo) & (kpos < hi), s, NEG)
                st[j] = s
                return jnp.maximum(m, fold(s, jnp.max))

            return step

        m = jnp.full((8, T), NEG, F32)
        m = lax.fori_loop(kb0, in0, score(True), m)
        m = lax.fori_loop(in0, in1, score(False), m)
        m = lax.fori_loop(in1, kb1, score(True), m)
        m = jnp.max(m, axis=0, keepdims=True)

        def weigh(j, carry):
            l, acc = carry
            p = jnp.exp(st[j] - m)
            l = l + fold(p, jnp.sum)
            acc = acc + jnp.dot(kvt_ref[j], p.astype(BF), preferred_element_type=F32)
            return l, acc

        l, acc = lax.fori_loop(kb0, kb1, weigh, (jnp.zeros((8, T), F32), jnp.zeros((2 * E, T), F32)))
        l = jnp.sum(l, axis=0, keepdims=True)
        out = acc[E:] / l
        att_ref[i] = out.astype(BF)
        wide = jnp.concatenate([out, jnp.zeros((E, T), F32)], axis=0).T
        edge_ref[i, 0] = wide[:8].astype(BF)
        edge_ref[i, 1] = wide[T - 8 :].astype(BF)
        lse_ref[i] = m + jnp.log(l)
        return 0

    lax.fori_loop(0, H, block, 0)


def forward(lens, kv, q):
    return pl.pallas_call(
        forward_kernel,
        name="attention_forward",
        out_shape=(
            jax.ShapeDtypeStruct((H, E, T), BF),
            jax.ShapeDtypeStruct((H, 2, 8, 2 * E), BF),
            jax.ShapeDtypeStruct((H, 1, T), F32),
            jax.ShapeDtypeStruct((NB, 2 * E, KB), BF),
        ),
        in_specs=[pl.BlockSpec(memory_space=pltpu.SMEM)] + vm(2),
        out_specs=tuple(vm(4)),
        scratch_shapes=[pltpu.VMEM((NB, KB, T), F32)],
    )(lens, kv.reshape(NB, KB, 2 * E), q)


def backward_kernel(len_ref, kv_ref, kvt_ref, q_ref, do_ref, att_ref, lse_ref, dq_ref, dkv_ref, acc_ref):
    part = lax.axis_index("ctx") % 4
    b = record_bounds(len_ref)

    def clear(j, _):
        acc_ref[j] = jnp.zeros((KB, 2 * E), F32)
        return 0

    lax.fori_loop(0, NB, clear, 0)

    def block(i, _):
        lo, hi, kb0, in0, in1, kb1 = block_span(i, part, b)
        qt, dot = q_ref[i], do_ref[i]
        rows = jnp.sum(dot.astype(F32) * att_ref[i].astype(F32), axis=0, keepdims=True)
        lse = lse_ref[i]
        zero = jnp.zeros((E, T), BF)
        both = jnp.concatenate(
            [jnp.concatenate([qt, zero], axis=0), jnp.concatenate([zero, dot], axis=0)], axis=1
        )
        back = both.astype(F32).T.astype(BF)

        def step(masked):
            def body(j, dq):
                sd = jnp.dot(kv_ref[j], both, preferred_element_type=F32)
                p = jnp.exp(sd[:, :T] - lse)
                if masked:
                    kpos = j * KB + lax.broadcasted_iota(jnp.int32, (KB, T), 0)
                    p = jnp.where((kpos >= lo) & (kpos < hi), p, 0.0)
                ds = (p * (sd[:, T:] - rows)).astype(BF)
                dq = dq + jnp.dot(kvt_ref[j], ds, preferred_element_type=F32)
                acc_ref[j] += jnp.dot(
                    jnp.concatenate([ds, p.astype(BF)], axis=1), back, preferred_element_type=F32
                )
                return dq

            return body

        dq = jnp.zeros((2 * E, T), F32)
        dq = lax.fori_loop(kb0, in0, step(True), dq)
        dq = lax.fori_loop(in0, in1, step(False), dq)
        dq = lax.fori_loop(in1, kb1, step(True), dq)
        dq_ref[i] = dq[:E].astype(BF)
        return 0

    lax.fori_loop(0, H, block, 0)

    def put(j, _):
        dkv_ref[j] = acc_ref[j].astype(BF)
        return 0

    lax.fori_loop(0, NB, put, 0)


def backward(lens, kv, kvt, q, do, att, lse):
    dq, dkv = pl.pallas_call(
        backward_kernel,
        name="attention_backward",
        out_shape=(
            jax.ShapeDtypeStruct((H, E, T), BF),
            jax.ShapeDtypeStruct((NB, KB, 2 * E), BF),
        ),
        in_specs=[pl.BlockSpec(memory_space=pltpu.SMEM)] + vm(6),
        out_specs=tuple(vm(2)),
        scratch_shapes=[pltpu.VMEM((NB, KB, 2 * E), F32)],
    )(lens, kv.reshape(NB, KB, 2 * E), kvt, q, do, att, lse)
    return dq, dkv.reshape(32, T, 2 * E)


def body(x, q, k, v, w, ck, lens, g):
    kv, qs, halo = gather_qkv(q, k, v, x, g)
    att, edge, lse, kvt = forward(lens, kv, qs)
    layer_output, input_grad, do, wg, kg = middle(lens, att, edge, x, g, halo, w, ck.astype(F32).T)
    dq, dkv = backward(lens, kv, kvt, qs, do, att, lse)
    dq, dk, dv, out_weight_grad, kg = spread_grads(dq, dkv, wg, kg)
    kernel_grad = jnp.transpose(kg[:, :9], (0, 2, 1)).reshape(1024, 9)
    return layer_output, input_grad, dq, dk, dv, out_weight_grad, kernel_grad


def solution(mesh):
    row = P(("dp", "ctx"), None)
    return jax.shard_map(
        body,
        mesh=mesh,
        in_specs=(row, row, row, row, P(), P(), P(), row),
        out_specs=(row, row, row, row, row, row, P()),
        check_vma=False,
    )
```

time: 244 us -> 153 us (0.63)
  blocking collectives: 79.6 us -> 0 us
  starting transfers between devices: 11.4 us -> 0 us
  local copies, waits for them, and re-layouts: 2.29 us -> 6.82 us
  other arithmetic: 5.71 us -> 1.39 us
  Pallas kernels: 140 us -> 144 us
  matrix products: 3.6 us -> 0 us
    psum x1 -> x0, blocking collectives: 79.6 us -> none  [body(): kernel_grad = lax.psum(jnp.stack(rows), ('dp', 'ctx')).T]
    pallas_call x4 -> x1, Pallas kernels: 47.1 us -> 22.7 us  [middle(): pl.pallas_call(mid_kernel, name='middle', out_shape=(jax.ShapeDtypeStruct...]
    pallas_call x1, Pallas kernels: 23.9 us -> 37.1 us  [spread_grads(): pl.pallas_call(spread_kernel, name='spread_grads', out_shape=(jax.ShapeDt...]
    ppermute x4 -> x0, starting transfers between devices: 11.4 us -> none  [the longest x2 8.77 us: with_sides(): before = lax.ppermute(x[-width:], 'ctx', up)]
    pallas_call x1, Pallas kernels: 23.1 us -> 31.1 us  [backward(): pl.pallas_call(backward_kernel, name='attention_backward', out_shape=(jax...]
    pallas_call x1, Pallas kernels: 19.2 us -> 26.2 us  [forward(): pl.pallas_call(forward_kernel, name='attention_forward', out_shape=(jax.S...]
    unnamed x15 -> x20, local copies, waits for them, and re-layouts: 0.65 us -> 5.92 us
    dot_general x3 -> x0, matrix products: 3.6 us -> none  [the longest x1 1.79 us: body(): lax.dot_general(input_grad, attended, (((0,), (0,)), ((), ())), preferred...]
  transfers between devices with their start and end apart: 4 -> 0, of which waited for: 0 -> 0; matrix products, arithmetic and copies ran while one was open for 1% -> 0% of each run, Pallas kernels for 0% -> 0%
where the time goes in v2:
time: 153 us
  Pallas kernels  144 us (94%)
  local copies, waits for them, and re-layouts  6.82 us (4%)
    pallas_call x1, Pallas kernels, spread_grads(): pl.pallas_call(spread_kernel, name='spread_grads', out_shape=(jax.ShapeDt...  37.1 us
    pallas_call x1, Pallas kernels, backward(): pl.pallas_call(backward_kernel, name='attention_backward', out_shape=(jax...  31.1 us
    pallas_call x1, Pallas kernels, gather_qkv(): pl.pallas_call(gather_kernel, name='gather_qkv', out_shape=(jax.ShapeDtyp...  26.8 us
    pallas_call x1, Pallas kernels, forward(): pl.pallas_call(forward_kernel, name='attention_forward', out_shape=(jax.S...  26.2 us
    pallas_call x1, Pallas kernels, middle(): pl.pallas_call(mid_kernel, name='middle', out_shape=(jax.ShapeDtypeStruct...  22.7 us
    unnamed x20, local copies, waits for them, and re-layouts  5.92 us

profile of v2, /device:TPU:1, one launch (start us, length us, event | category | flops | bytes accessed | tf_op | source)
XLA Modules:
  0.0 152.8 jit_solution(3231621603132649240)
XLA Ops:
  0.6 1.4 convert_bitcast_fusion.ck_ref
  2.0 26.8 %gather_qkv.1 = (bf16[32,128,128]{2,1,0:T(8,128)(2,1)}, bf16[8,64,128]{2,1,0:T(8,128)(2,1)}, bf16[2,2,8,1024]{3,2,1,0:T(8,128)(2,1)}) custom-call(bf16[128,512]{1,0:T(8,128)(2,1)} %q_ref.1, bf16[128,512]{1,0:T(8,128)(2,1)} %k_ref.1, bf16[128,512]{1,0:T(8,128)(2,1)} %v_ref.1, bf16[128,1024]{1,0:T(8,128)(2,1)} %x_ref.3, bf16[128,1024]{1,0:T(8,128)(2,1)} %g_ref.3), custom_call_target="tpu_custom_call" | custom-call | tf_op jit(solution)/shard_map/gather_qkv/pallas_call | solution.py:125
  28.9 26.2 %attention_forward.1 = (bf16[8,64,128]{2,1,0:T(8,128)(2,1)}, bf16[8,2,8,128]{3,2,1,0:T(8,128)(2,1)}, f32[8,1,128]{2,1,0:T(1,128)}, bf16[16,128,256]{2,1,0:T(8,128)(2,1)}) custom-call(s32[4,4]{1,0:T(4,128)} %len_ref.5, bf16[16,256,128]{2,1,0:T(8,128)(2,1)} %bitcast.13, bf16[8,64,128]{2,1,0:T(8,128)(2,1)} %get-tuple-element.27.q_ref), custom_call_target="tpu_custom_call" | custom-call | tf_op jit(solution)/shard_map/attention_forward/pallas_call | solution.py:611
  55.0 22.7 %middle.1 = (bf16[128,1024]{1,0:T(8,128)(2,1)}, bf16[128,1024]{1,0:T(8,128)(2,1)}, bf16[8,64,128]{2,1,0:T(8,128)(2,1)}, bf16[64,8,512]{2,1,0:T(8,128)(2,1)}, f32[8,16,128]{2,1,0:T(8,128)}) custom-call(s32[4,4]{1,0:T(4,128)} %len_ref.5, bf16[8,64,128]{2,1,0:T(8,128)(2,1)} %get-tuple-element.28.att_ref, bf16[8,2,8,128]{3,2,1,0:T(8,128)(2,1)} %get-tuple-element.29.edge_ref, ...), custom_call_target="tpu_custom_call" | custom-call | tf_op jit(solution)/shard_map/middle/pallas_call | solution.py:338
  77.8 31.1 %attention_backward.1 = (bf16[8,64,128]{2,1,0:T(8,128)(2,1)}, bf16[16,256,128]{2,1,0:T(8,128)(2,1)}) custom-call(s32[4,4]{1,0:T(4,128)} %len_ref.5, bf16[16,256,128]{2,1,0:T(8,128)(2,1)} %bitcast.14, bf16[16,128,256]{2,1,0:T(8,128)(2,1)} %get-tuple-element.33.kvt_ref, bf16[8,64,128]{2,1,0:T(8,128)(2,1)} %get-tuple-element.27.q_ref, ...), custom_call_target="tpu_custom_call" | custom-call | tf_op jit(solution)/shard_map/attention_backward/pallas_call | solution.py:680
  108.9 37.1 %spread_grads.1 = (bf16[128,512]{1,0:T(8,128)(2,1)}, bf16[128,512]{1,0:T(8,128)(2,1)}, bf16[128,512]{1,0:T(8,128)(2,1)}, f32[8,512]{1,0:T(8,128)}, f32[8,16,128]{2,1,0:T(8,128)}) custom-call(bf16[8,64,128]{2,1,0:T(8,128)(2,1)} %get-tuple-element.36.dq_ref, bf16[32,128,128]{2,1,0:T(8,128)(2,1)} %bitcast.15, bf16[64,8,512]{2,1,0:T(8,128)(2,1)} %get-tuple-element.38.wg_ref, ...), custom_call_target="tpu_custom_call" | custom-call | tf_op jit(solution)/shard_map/spread_grads/pallas_call | solution.py:489
  146.0 0.0 copy-start.1
  146.0 0.9 slice_bitcast_fusion
  146.9 0.6 copy.16
  147.5 0.0 copy-done.1
  147.5 0.0 copy-start
  147.5 0.7 copy.25
  148.2 0.3 copy-done
  148.6 0.0 copy-start.4
  148.6 0.7 copy.26
  149.3 0.3 copy-done.4
  149.6 0.0 copy-start.3
  149.6 0.7 copy.27
  150.2 0.3 copy-done.3
  150.5 0.7 copy.28
  151.2 0.3 copy-done.2
  151.5 0.7 copy.29
  152.1 0.1 copy-done.5
  152.2 0.6 copy.30
  (4 shorter events, 0.0 us)
Async XLA Ops:
  146.0 1.6 %copy-start.1 = (bf16[128,1024]{1,0:T(8,128)(2,1)S(1)}, bf16[128,1024]{1,0:T(8,128)(2,1)}, u32[]{:S(2)}) copy-start(bf16[128,1024]{1,0:T(8,128)(2,1)} %get-tuple-element.52) | copy-start | bytes 786436
  147.5 1.0 copy-start
  148.6 1.0 copy-start.4
  149.6 1.0 copy-start.3
  150.5 1.0 copy-start.2
  151.5 0.7 copy-start.5

commit v3 on v2

--- a/solution.py
+++ b/solution.py
@@ -17,6 +17,7 @@
 T = 128
 KB = 256
 NB = 4096 // KB
+U = 4
 
 
 def vm(n):
@@ -527,28 +528,57 @@
     return s1, s2, s3, s3 + len_ref[g, 3]
 
 
-def low_of(pos, b):
-    return jnp.where(pos >= b[2], b[2], jnp.where(pos >= b[1], b[1], jnp.where(pos >= b[0], b[0], 0)))
-
-
-def high_of(pos, b):
-    return jnp.where(pos < b[0], b[0], jnp.where(pos < b[1], b[1], jnp.where(pos < b[2], b[2], b[3])))
-
-
-def block_span(i, part, b):
-    f0 = (i * 4 + part) * T
-    pos = f0 + lax.broadcasted_iota(jnp.int32, (1, T), 1)
-    lo, hi = low_of(pos, b), high_of(pos, b)
-    first_lo, first_hi = low_of(f0, b), high_of(f0, b)
-    last_hi = high_of(f0 + T - 1, b)
-    kb0 = first_lo // KB
-    kb1 = (last_hi + KB - 1) // KB
-    same = first_hi == last_hi
-    in0 = jnp.where(same, (first_lo + KB - 1) // KB, kb1)
-    in1 = jnp.where(same, first_hi // KB, kb1)
-    in0 = jnp.minimum(in0, kb1)
-    in1 = jnp.maximum(in1, in0)
-    return lo, hi, kb0, in0, in1, kb1
+def record_of(pos, b):
+    one = lambda s: jnp.where(pos >= s, 1, 0)
+    return one(b[0]) + one(b[1]) + one(b[2])
+
+
+def prepare_keys(b, kv_ref, kx, kt):
+    def turn(j, _):
+        kv = kv_ref[j]
+        kt[j] = kv.astype(F32).T.astype(BF)
+        kx[j, :, : 2 * E] = kv
+        pos = j * KB + lax.broadcasted_iota(jnp.int32, (KB, 2 * E), 0)
+        lane = lax.broadcasted_iota(jnp.int32, (KB, 2 * E), 1)
+        kx[j, :, 2 * E :] = jnp.where(record_of(pos, b) == lane, 1.0, 0.0).astype(BF)
+        return 0
+
+    lax.fori_loop(0, NB, turn, 0)
+
+
+def other_records(i, part, b):
+    pos = (i * 4 + part) * T + lax.broadcasted_iota(jnp.int32, (2 * E, T), 1)
+    row = lax.broadcasted_iota(jnp.int32, (2 * E, T), 0)
+    return jnp.where((row < 4) & (record_of(pos, b) != row), NEG, 0.0).astype(BF)
+
+
+def plan_blocks(part, b, first, last):
+    count = jnp.int32(0)
+    for i in range(H):
+        f0 = (i * 4 + part) * T
+        f1 = f0 + T - 1
+        lo = jnp.where(f0 >= b[2], b[2], jnp.where(f0 >= b[1], b[1], jnp.where(f0 >= b[0], b[0], 0)))
+        hi = jnp.where(f1 < b[0], b[0], jnp.where(f1 < b[1], b[1], jnp.where(f1 < b[2], b[2], b[3])))
+        first[i] = lo // KB
+        last[i] = (hi + KB - 1) // KB
+        count = count + last[i] - first[i]
+    first[H] = jnp.int32(0)
+    last[H] = jnp.int32(1 << 20)
+    return count
+
+
+def run_items(count, first, last, item):
+    def step(t, carry):
+        i, kb = carry
+        for u in range(U):
+            item(t * U + u, i, kb)
+            more = kb + 1 < last[i]
+            after = jnp.minimum(i + 1, H)
+            kb = jnp.where(more, kb + 1, first[after])
+            i = jnp.where(more, i, after)
+        return i, kb
+
+    lax.fori_loop(0, (count + U - 1) // U, step, (jnp.int32(0), first[0]))
 
 
 def fold(x, op):
@@ -556,55 +586,42 @@
     return op(r, axis=0)
 
 
-def forward_kernel(len_ref, kv_ref, q_ref, att_ref, edge_ref, lse_ref, kvt_ref, st):
+def forward_kernel(len_ref, kv_ref, q_ref, att_ref, edge_ref, lse_ref, kx, kt, qa, st, m8, m1, l8, acc, first, last):
     part = lax.axis_index("ctx") % 4
     b = record_bounds(len_ref)
-
-    def turn(j, _):
-        kvt_ref[j] = kv_ref[j].astype(F32).T.astype(BF)
-        return 0
-
-    lax.fori_loop(0, NB, turn, 0)
-
-    def block(i, _):
-        lo, hi, kb0, in0, in1, kb1 = block_span(i, part, b)
-        qz = jnp.concatenate([q_ref[i], jnp.zeros((E, T), BF)], axis=0)
-
-        def score(masked):
-            def step(j, m):
-                s = jnp.dot(kv_ref[j], qz, preferred_element_type=F32)
-                if masked:
-                    kpos = j * KB + lax.broadcasted_iota(jnp.int32, (KB, T), 0)
-                    s = jnp.where((kpos >= lo) & (kpos < hi), s, NEG)
-                st[j] = s
-                return jnp.maximum(m, fold(s, jnp.max))
-
-            return step
-
-        m = jnp.full((8, T), NEG, F32)
-        m = lax.fori_loop(kb0, in0, score(True), m)
-        m = lax.fori_loop(in0, in1, score(False), m)
-        m = lax.fori_loop(in1, kb1, score(True), m)
-        m = jnp.max(m, axis=0, keepdims=True)
-
-        def weigh(j, carry):
-            l, acc = carry
-            p = jnp.exp(st[j] - m)
-            l = l + fold(p, jnp.sum)
-            acc = acc + jnp.dot(kvt_ref[j], p.astype(BF), preferred_element_type=F32)
-            return l, acc
-
-        l, acc = lax.fori_loop(kb0, kb1, weigh, (jnp.zeros((8, T), F32), jnp.zeros((2 * E, T), F32)))
-        l = jnp.sum(l, axis=0, keepdims=True)
-        out = acc[E:] / l
+    count = plan_blocks(part, b, first, last)
+    prepare_keys(b, kv_ref, kx, kt)
+    for i in range(H):
+        qa[i, :E] = q_ref[i]
+        qa[i, E : 2 * E] = jnp.zeros((E, T), BF)
+        qa[i, 2 * E :] = other_records(i, part, b)
+    qa[H] = jnp.zeros((4 * E, T), BF)
+    m8[...] = jnp.full((H + 1, 8, T), NEG, F32)
+    l8[...] = jnp.zeros((H + 1, 8, T), F32)
+    acc[...] = jnp.zeros((H + 1, 2 * E, T), F32)
+
+    def score(t, i, kb):
+        s = jnp.dot(kx[kb], qa[i], preferred_element_type=F32)
+        st[t] = s
+        m8[i] = jnp.maximum(m8[i], fold(s, jnp.max))
+
+    run_items(count, first, last, score)
+    m1[...] = jnp.max(m8[...], axis=1, keepdims=True)
+
+    def weigh(t, i, kb):
+        p = jnp.exp(st[t] - m1[i])
+        l8[i] += fold(p, jnp.sum)
+        acc[i] += jnp.dot(kt[kb], p.astype(BF), preferred_element_type=F32)
+
+    run_items(count, first, last, weigh)
+    l1 = jnp.sum(l8[...], axis=1, keepdims=True)
+    lse_ref[...] = m1[:H] + jnp.log(l1[:H])
+    for i in range(H):
+        out = acc[i, E:] / l1[i]
         att_ref[i] = out.astype(BF)
         wide = jnp.concatenate([out, jnp.zeros((E, T), F32)], axis=0).T
         edge_ref[i, 0] = wide[:8].astype(BF)
         edge_ref[i, 1] = wide[T - 8 :].astype(BF)
-        lse_ref[i] = m + jnp.log(l)
-        return 0
-
-    lax.fori_loop(0, H, block, 0)
 
 
 def forward(lens, kv, q):
@@ -615,68 +632,72 @@
             jax.ShapeDtypeStruct((H, E, T), BF),
             jax.ShapeDtypeStruct((H, 2, 8, 2 * E), BF),
             jax.ShapeDtypeStruct((H, 1, T), F32),
-            jax.ShapeDtypeStruct((NB, 2 * E, KB), BF),
         ),
         in_specs=[pl.BlockSpec(memory_space=pltpu.SMEM)] + vm(2),
-        out_specs=tuple(vm(4)),
-        scratch_shapes=[pltpu.VMEM((NB, KB, T), F32)],
+        out_specs=tuple(vm(3)),
+        scratch_shapes=[
+            pltpu.VMEM((NB, KB, 4 * E), BF),
+            pltpu.VMEM((NB, 2 * E, KB), BF),
+            pltpu.VMEM((H + 1, 4 * E, T), BF),
+            pltpu.VMEM((H * NB + U, KB, T), F32),
+            pltpu.VMEM((H + 1, 8, T), F32),
+            pltpu.VMEM((H + 1, 1, T), F32),
+            pltpu.VMEM((H + 1, 8, T), F32),
+            pltpu.VMEM((H + 1, 2 * E, T), F32),
+            pltpu.SMEM((H + 1,), jnp.int32),
+            pltpu.SMEM((H + 1,), jnp.int32),
+        ],
     )(lens, kv.reshape(NB, KB, 2 * E), q)
 
 
-def backward_kernel(len_ref, kv_ref, kvt_ref, q_ref, do_ref, att_ref, lse_ref, dq_ref, dkv_ref, acc_ref):
+def backward_kernel(
+    len_ref, kv_ref, q_ref, do_ref, att_ref, lse_ref, dq_ref, dkv_ref,
+    kx, kt, both, back, lse, rows, dq, acc, first, last,
+):
     part = lax.axis_index("ctx") % 4
     b = record_bounds(len_ref)
-
-    def clear(j, _):
-        acc_ref[j] = jnp.zeros((KB, 2 * E), F32)
-        return 0
-
-    lax.fori_loop(0, NB, clear, 0)
-
-    def block(i, _):
-        lo, hi, kb0, in0, in1, kb1 = block_span(i, part, b)
+    count = plan_blocks(part, b, first, last)
+    prepare_keys(b, kv_ref, kx, kt)
+    acc[...] = jnp.zeros((NB, KB, 2 * E), F32)
+    dq[...] = jnp.zeros((H + 1, 2 * E, T), F32)
+    zero = jnp.zeros((E, T), BF)
+    for i in range(H):
         qt, dot = q_ref[i], do_ref[i]
-        rows = jnp.sum(dot.astype(F32) * att_ref[i].astype(F32), axis=0, keepdims=True)
-        lse = lse_ref[i]
-        zero = jnp.zeros((E, T), BF)
-        both = jnp.concatenate(
+        rows[i] = jnp.sum(dot.astype(F32) * att_ref[i].astype(F32), axis=0, keepdims=True)
+        lse[i] = lse_ref[i]
+        pair = jnp.concatenate(
             [jnp.concatenate([qt, zero], axis=0), jnp.concatenate([zero, dot], axis=0)], axis=1
         )
-        back = both.astype(F32).T.astype(BF)
-
-        def step(masked):
-            def body(j, dq):
-                sd = jnp.dot(kv_ref[j], both, preferred_element_type=F32)
-                p = jnp.exp(sd[:, :T] - lse)
-                if masked:
-                    kpos = j * KB + lax.broadcasted_iota(jnp.int32, (KB, T), 0)
-                    p = jnp.where((kpos >= lo) & (kpos < hi), p, 0.0)
-                ds = (p * (sd[:, T:] - rows)).astype(BF)
-                dq = dq + jnp.dot(kvt_ref[j], ds, preferred_element_type=F32)
-                acc_ref[j] += jnp.dot(
-                    jnp.concatenate([ds, p.astype(BF)], axis=1), back, preferred_element_type=F32
-                )
-                return dq
-
-            return body
-
-        dq = jnp.zeros((2 * E, T), F32)
-        dq = lax.fori_loop(kb0, in0, step(True), dq)
-        dq = lax.fori_loop(in0, in1, step(False), dq)
-        dq = lax.fori_loop(in1, kb1, step(True), dq)
-        dq_ref[i] = dq[:E].astype(BF)
-        return 0
-
-    lax.fori_loop(0, H, block, 0)
+        both[i, : 2 * E] = pair
+        both[i, 2 * E :, :T] = other_records(i, part, b)
+        both[i, 2 * E :, T:] = jnp.zeros((2 * E, T), BF)
+        back[i] = pair.astype(F32).T.astype(BF)
+    rows[H] = jnp.zeros((1, T), F32)
+    lse[H] = jnp.zeros((1, T), F32)
+    both[H] = jnp.zeros((4 * E, 2 * T), BF)
+    back[H] = jnp.zeros((2 * T, 2 * E), BF)
+
+    def item(t, i, kb):
+        sd = jnp.dot(kx[kb], both[i], preferred_element_type=F32)
+        p = jnp.exp(sd[:, :T] - lse[i])
+        ds = (p * (sd[:, T:] - rows[i])).astype(BF)
+        dq[i] += jnp.dot(kt[kb], ds, preferred_element_type=F32)
+        acc[kb] += jnp.dot(
+            jnp.concatenate([ds, p.astype(BF)], axis=1), back[i], preferred_element_type=F32
+        )
+
+    run_items(count, first, last, item)
+    for i in range(H):
+        dq_ref[i] = dq[i, :E].astype(BF)
 
     def put(j, _):
-        dkv_ref[j] = acc_ref[j].astype(BF)
+        dkv_ref[j] = acc[j].astype(BF)
         return 0
 
     lax.fori_loop(0, NB, put, 0)
 
 
-def backward(lens, kv, kvt, q, do, att, lse):
+def backward(lens, kv, q, do, att, lse):
     dq, dkv = pl.pallas_call(
         backward_kernel,
         name="attention_backward",
@@ -684,18 +705,29 @@
             jax.ShapeDtypeStruct((H, E, T), BF),
             jax.ShapeDtypeStruct((NB, KB, 2 * E), BF),
         ),
-        in_specs=[pl.BlockSpec(memory_space=pltpu.SMEM)] + vm(6),
+        in_specs=[pl.BlockSpec(memory_space=pltpu.SMEM)] + vm(5),
         out_specs=tuple(vm(2)),
-        scratch_shapes=[pltpu.VMEM((NB, KB, 2 * E), F32)],
-    )(lens, kv.reshape(NB, KB, 2 * E), kvt, q, do, att, lse)
+        scratch_shapes=[
+            pltpu.VMEM((NB, KB, 4 * E), BF),
+            pltpu.VMEM((NB, 2 * E, KB), BF),
+            pltpu.VMEM((H + 1, 4 * E, 2 * T), BF),
+            pltpu.VMEM((H + 1, 2 * T, 2 * E), BF),
+            pltpu.VMEM((H + 1, 1, T), F32),
+            pltpu.VMEM((H + 1, 1, T), F32),
+            pltpu.VMEM((H + 1, 2 * E, T), F32),
+            pltpu.VMEM((NB, KB, 2 * E), F32),
+            pltpu.SMEM((H + 1,), jnp.int32),
+            pltpu.SMEM((H + 1,), jnp.int32),
+        ],
+    )(lens, kv.reshape(NB, KB, 2 * E), q, do, att, lse)
     return dq, dkv.reshape(32, T, 2 * E)
 
 
 def body(x, q, k, v, w, ck, lens, g):
     kv, qs, halo = gather_qkv(q, k, v, x, g)
-    att, edge, lse, kvt = forward(lens, kv, qs)
+    att, edge, lse = forward(lens, kv, qs)
     layer_output, input_grad, do, wg, kg = middle(lens, att, edge, x, g, halo, w, ck.astype(F32).T)
-    dq, dkv = backward(lens, kv, kvt, qs, do, att, lse)
+    dq, dkv = backward(lens, kv, qs, do, att, lse)
     dq, dk, dv, out_weight_grad, kg = spread_grads(dq, dkv, wg, kg)
     kernel_grad = jnp.transpose(kg[:, :9], (0, 2, 1)).reshape(1024, 9)
     return layer_output, input_grad, dq, dk, dv, out_weight_grad, kernel_grad

time: 153 us -> 130 us (0.85)
  Pallas kernels: 144 us -> 121 us
    pallas_call x1, Pallas kernels: 31.1 us -> 16.2 us  [backward(): pl.pallas_call(backward_kernel, name='attention_backward', out_shape=(jax...]
    pallas_call x1, Pallas kernels: 26.2 us -> 12.2 us  [forward(): pl.pallas_call(forward_kernel, name='attention_forward', out_shape=(jax.S...]
    pallas_call x1, Pallas kernels: 37.1 us -> 40.9 us  [spread_grads(): pl.pallas_call(spread_kernel, name='spread_grads', out_shape=(jax.ShapeDt...]
    pallas_call x1, Pallas kernels: 22.7 us -> 24.9 us  [middle(): pl.pallas_call(mid_kernel, name='middle', out_shape=(jax.ShapeDtypeStruct...]
where the time goes in v3:
time: 130 us
  Pallas kernels  121 us (93%)
  local copies, waits for them, and re-layouts  6.82 us (5%)
  other arithmetic  1.39 us (1%)
    pallas_call x1, Pallas kernels, spread_grads(): pl.pallas_call(spread_kernel, name='spread_grads', out_shape=(jax.ShapeDt...  40.9 us
    pallas_call x1, Pallas kernels, gather_qkv(): pl.pallas_call(gather_kernel, name='gather_qkv', out_shape=(jax.ShapeDtyp...  26.8 us
    pallas_call x1, Pallas kernels, middle(): pl.pallas_call(mid_kernel, name='middle', out_shape=(jax.ShapeDtypeStruct...  24.9 us
    pallas_call x1, Pallas kernels, backward(): pl.pallas_call(backward_kernel, name='attention_backward', out_shape=(jax...  16.2 us
    pallas_call x1, Pallas kernels, forward(): pl.pallas_call(forward_kernel, name='attention_forward', out_shape=(jax.S...  12.2 us
    unnamed x20, local copies, waits for them, and re-layouts  5.92 us

profile of v3, /device:TPU:1, one launch (start us, length us, event | category | flops | bytes accessed | tf_op | source)
XLA Modules:
  0.0 129.8 jit_solution(1282689035831264090)
XLA Ops:
  0.6 1.4 %convert_bitcast_fusion.ck_ref = f32[9,1024]{1,0:T(8,128)} fusion(bf16[1024,9]{0,1:T(8,128)(2,1)} %param.13), kind=kLoop, calls=%fused_computation | loop fusion | flops 9216 | bytes 55296 | tf_op jit(solution)/shard_map/transpose | solution.py:729
  2.0 26.8 %gather_qkv.1 = (bf16[32,128,128]{2,1,0:T(8,128)(2,1)}, bf16[8,64,128]{2,1,0:T(8,128)(2,1)}, bf16[2,2,8,1024]{3,2,1,0:T(8,128)(2,1)}) custom-call(bf16[128,512]{1,0:T(8,128)(2,1)} %q_ref.1, bf16[128,512]{1,0:T(8,128)(2,1)} %k_ref.1, bf16[128,512]{1,0:T(8,128)(2,1)} %v_ref.1, bf16[128,1024]{1,0:T(8,128)(2,1)} %x_ref.3, bf16[128,1024]{1,0:T(8,128)(2,1)} %g_ref.3), custom_call_target="tpu_custom_call" | custom-call | tf_op jit(solution)/shard_map/gather_qkv/pallas_call | solution.py:126
  28.9 12.2 %attention_forward.1 = (bf16[8,64,128]{2,1,0:T(8,128)(2,1)}, bf16[8,2,8,128]{3,2,1,0:T(8,128)(2,1)}, f32[8,1,128]{2,1,0:T(1,128)}) custom-call(s32[4,4]{1,0:T(4,128)} %len_ref.5, bf16[16,256,128]{2,1,0:T(8,128)(2,1)} %bitcast.13, bf16[8,64,128]{2,1,0:T(8,128)(2,1)} %get-tuple-element.26.q_ref), custom_call_target="tpu_custom_call" | custom-call | tf_op jit(solution)/shard_map/attention_forward/pallas_call | solution.py:628
  41.1 24.9 %middle.1 = (bf16[128,1024]{1,0:T(8,128)(2,1)}, bf16[128,1024]{1,0:T(8,128)(2,1)}, bf16[8,64,128]{2,1,0:T(8,128)(2,1)}, bf16[64,8,512]{2,1,0:T(8,128)(2,1)}, f32[8,16,128]{2,1,0:T(8,128)}) custom-call(s32[4,4]{1,0:T(4,128)} %len_ref.5, bf16[8,64,128]{2,1,0:T(8,128)(2,1)} %get-tuple-element.27.att_ref, bf16[8,2,8,128]{3,2,1,0:T(8,128)(2,1)} %get-tuple-element.28.edge_ref, ...), custom_call_target="tpu_custom_call" | custom-call | tf_op jit(solution)/shard_map/middle/pallas_call | solution.py:339
  65.9 16.2 %attention_backward.1 = (bf16[8,64,128]{2,1,0:T(8,128)(2,1)}, bf16[16,256,128]{2,1,0:T(8,128)(2,1)}) custom-call(s32[4,4]{1,0:T(4,128)} %len_ref.5, bf16[16,256,128]{2,1,0:T(8,128)(2,1)} %bitcast.14, bf16[8,64,128]{2,1,0:T(8,128)(2,1)} %get-tuple-element.26.q_ref, bf16[8,64,128]{2,1,0:T(8,128)(2,1)} %get-tuple-element.32.do_ref, ...), custom_call_target="tpu_custom_call" | custom-call | tf_op jit(solution)/shard_map/attention_backward/pallas_call | solution.py:701
  82.1 40.9 %spread_grads.1 = (bf16[128,512]{1,0:T(8,128)(2,1)}, bf16[128,512]{1,0:T(8,128)(2,1)}, bf16[128,512]{1,0:T(8,128)(2,1)}, f32[8,512]{1,0:T(8,128)}, f32[8,16,128]{2,1,0:T(8,128)}) custom-call(bf16[8,64,128]{2,1,0:T(8,128)(2,1)} %get-tuple-element.34.dq_ref, bf16[32,128,128]{2,1,0:T(8,128)(2,1)} %bitcast.15, bf16[64,8,512]{2,1,0:T(8,128)(2,1)} %get-tuple-element.36.wg_ref, ...), custom_call_target="tpu_custom_call" | custom-call | tf_op jit(solution)/shard_map/spread_grads/pallas_call | solution.py:490
  123.0 0.0 copy-start.1
  123.0 0.9 slice_bitcast_fusion
  123.9 0.6 copy.16
  124.6 0.0 copy-done.1
  124.6 0.0 copy-start
  124.6 0.7 copy.25
  125.3 0.3 copy-done
  125.6 0.0 copy-start.4
  125.6 0.7 copy.26
  126.3 0.3 copy-done.4
  126.6 0.0 copy-start.3
  126.6 0.7 copy.27
  127.3 0.3 copy-done.3
  127.6 0.7 copy.28
  128.2 0.3 copy-done.2
  128.5 0.7 copy.29
  129.2 0.1 copy-done.5
  129.2 0.6 copy.30
  (4 shorter events, 0.0 us)
Async XLA Ops:
  123.0 1.6 %copy-start.1 = (bf16[128,1024]{1,0:T(8,128)(2,1)S(1)}, bf16[128,1024]{1,0:T(8,128)(2,1)}, u32[]{:S(2)}) copy-start(bf16[128,1024]{1,0:T(8,128)(2,1)} %get-tuple-element.50) | copy-start | bytes 786436
  124.6 1.0 copy-start
  125.6 1.0 copy-start.4
  126.6 1.0 copy-start.3
  127.6 1.0 copy-start.2
  128.5 0.7 copy-start.5

commit v4 on v0

v4 whole, which is shorter than its diff:
```python
import jax
import jax.numpy as jnp
from jax import lax
from jax.experimental import pallas as pl
from jax.experimental.pallas import tpu as pltpu
from jax.sharding import PartitionSpec as P

MESH = pl.DeviceIdType.MESH
BF = jnp.bfloat16
F32 = jnp.float32
H = 8
E = 64
C = 1024
SCALE = 0.125
NEG = -1e30
T = 128
KB = 256
NB = 16
NT = (((1,), (1,)), ((), ()))
TN = (((0,), (0,)), ((), ()))


def vm(n):
    return [pl.BlockSpec(memory_space=pltpu.VMEM)] * n


def loop(a, b, f):
    def step(d, _):
        f(d)
        return 0

    lax.fori_loop(a, b, step, 0)


def fold(x, op):
    return op(x.reshape(x.shape[0] // 8, 8, x.shape[1]), axis=0)


def remote(src, dst, snd, rcv, where):
    return pltpu.make_async_remote_copy(
        src_ref=src, dst_ref=dst, send_sem=snd, recv_sem=rcv, device_id=where, device_id_type=MESH
    )


def layer_kernel(
    len_ref, q_ref, k_ref, v_ref, x_ref, g_ref, w_ref, ck_ref,
    lo_ref, ig_ref, dq_ref, dk_ref, dv_ref, wo_ref, ko_ref,
    kvs, qs, kv_in, q_in, halo, kx, kt, both, back, m1, l8, acc, lse, rows, att, edge,
    at_in, eb, am, ap, igs, igp, dos, do_in, mx, ge, cs, mk, cf, wg, wg_in,
    kg, k1, k2, ksum, kall, dsp, dqa, dks, dkv_in, dqs, dq_in,
    kv_s, kv_r, q_s, q_r, h_s, h_r, a_s, a_r, e_s, e_r, d_s, d_r, p_s, p_r,
    w_s, w_r, k1_s, k1_r, k2_s, k2_r, k3_s, k3_r, g_s, g_r, y_s, y_r,
):
    dp, me = lax.axis_index("dp"), lax.axis_index("ctx")
    core, part, plane = dp % 2, me % 4, me // 4
    partner = {"dp": dp - core + (1 - core)}
    chip = (dp // 2) * 32 + me

    def plane_at(d):
        return {"ctx": (me + 4 * d) % 32}

    def chip_at(d):
        other = (chip + d) % 64
        return {"dp": (other // 32) * 2 + core, "ctx": other % 32}

    def column_at(d):
        other = (dp * 4 + part + d) % 16
        return {"dp": other // 4, "ctx": plane * 4 + other % 4}

    barrier = pltpu.get_barrier_semaphore()

    def signal(where):
        pl.semaphore_signal(barrier, inc=1, device_id=where, device_id_type=MESH)

    loop(1, 64, lambda d: signal(chip_at(d)))
    loop(0, 8, lambda d: signal({"dp": (d // 4) * 2 + 1 - core, "ctx": plane * 4 + d % 4}))

    for h in range(H):
        cols = slice(h * E, (h + 1) * E)
        kvs[h] = jnp.concatenate([k_ref[:, cols], v_ref[:, cols]], axis=1)
    qt = (q_ref[...].astype(F32) * SCALE).T.astype(BF)
    for h in range(H):
        qs[h] = qt[h * E : (h + 1) * E, :]
    kv_in[0] = kvs[plane]
    q_in[0] = qs[plane]

    s1 = len_ref[dp, 0]
    s2 = s1 + len_ref[dp, 1]
    s3 = s2 + len_ref[dp, 2]
    s4 = s3 + len_ref[dp, 3]

    def record_of(pos):
        one = lambda s: jnp.where(pos >= s, 1, 0)
        return one(s1) + one(s2) + one(s3)

    pl.semaphore_wait(barrier, 71)

    q_copy = lambda d: remote(qs.at[(plane + d) % 8], q_in.at[d], q_s.at[d], q_r.at[d], plane_at(d))
    kv_copy = lambda d: remote(
        kvs.at[((me + d) % 32) // 4], kv_in.at[d], kv_s.at[d], kv_r.at[d], {"ctx": (me + d) % 32}
    )

    def halo_copy(a, up):
        ref, s = (x_ref, g_ref)[a], 0 if up else 1
        return remote(
            ref.at[pl.ds(T - 8, 8)] if up else ref.at[pl.ds(0, 8)],
            halo.at[a, s],
            h_s.at[a, s],
            h_r.at[a, s],
            {"ctx": (me + (1 if up else 31)) % 32},
        )

    halos = [halo_copy(a, up) for a in range(2) for up in (True, False)]
    loop(1, 8, lambda d: q_copy(d).start())
    loop(1, 32, lambda d: kv_copy(d).start())
    for c in halos:
        c.start()

    m1[...] = jnp.full((H, 1, T), NEG, F32)
    l8[...] = jnp.zeros((H, 8, T), F32)
    acc[...] = jnp.zeros((H, E, T), F32)
    lane = lax.broadcasted_iota(jnp.int32, (1, 2 * E), 1)
    pick = lambda a, b, c, d, e: jnp.where(
        lane == 0, a, jnp.where(lane == 1, b, jnp.where(lane == 2, c, jnp.where(lane == 3, d, e)))
    )
    begin, end = pick(0, s1, s2, s3, s4), pick(s1, s2, s3, s4, s4)

    for i in range(H):
        pos = (i * 4 + part) * T + lax.broadcasted_iota(jnp.int32, (2 * E, T), 1)
        row = lax.broadcasted_iota(jnp.int32, (2 * E, T), 0)
        both[i, : 2 * E] = jnp.zeros((2 * E, 2 * T), BF)
        both[i, 2 * E :, :T] = jnp.where((row < 4) & (record_of(pos) != row), NEG, 0.0).astype(BF)
        both[i, 2 * E :, T:] = jnp.zeros((2 * E, T), BF)

    pos = me * T - 4 + lax.broadcasted_iota(jnp.int32, (136, 128), 0)
    label = lambda p: jnp.where((p >= 0) & (p < s4), record_of(p), -1)
    mine = label(pos)
    for j in range(9):
        mk[j] = jnp.where(label(pos + (j - 4)) == mine, 1.0, 0.0)
    cf[0:9] = ck_ref[...].astype(F32)
    ge[8:136] = g_ref[...].astype(F32)

    loop(1, 8, lambda d: q_copy(d).wait_recv())
    for i in range(H):
        both[i, :E, :T] = q_in[(plane - i + 8) % 8]

    def arrive(d):
        kv_copy(d).wait_recv()

    def forward_step(t):
        @pl.when(t > 0)
        def _():
            arrive(2 * t)

        arrive(2 * t + 1)
        for u in range(2):
            kv = kv_in[2 * t + u]
            kt[t, :, u * T : (u + 1) * T] = kv.astype(F32).T.astype(BF)
            at = slice(u * T, (u + 1) * T)
            kx[t, at, : 2 * E] = kv
            p = (me - 2 * t - u + 32) % 32 * T + lax.broadcasted_iota(jnp.int32, (T, 2 * E), 0)
            kx[t, at, 2 * E :] = jnp.where((p >= begin) & (p < end), 1.0, 0.0).astype(BF)
        for i in range(H):
            s = jnp.dot(kx[t], both[i, :, :T], preferred_element_type=F32)
            old = m1[i]
            new = jnp.maximum(old, jnp.max(fold(s, jnp.max), axis=0, keepdims=True))
            p = jnp.exp(s - new)
            scale = jnp.exp(old - new)
            m1[i] = new
            l8[i] = l8[i] * scale + fold(p, jnp.sum)
            acc[i] = acc[i] * scale + jnp.dot(kt[t, E:], p.astype(BF), preferred_element_type=F32)

    loop(0, NB, forward_step)
    for i in range(H):
        total = jnp.sum(l8[i], axis=0, keepdims=True)
        lse[i] = m1[i] + jnp.log(total)
        out = acc[i] / total
        att[i] = out.astype(BF)
        wide = jnp.concatenate([out, jnp.zeros((E, T), F32)], axis=0).T
        edge[i, 0] = wide[:8].astype(BF)
        edge[i, 1] = wide[T - 8 :].astype(BF)

    a_copy = lambda d: remote(att.at[(plane + d) % 8], at_in.at[plane], a_s.at[d], a_r.at[d], plane_at(d))

    def e_copy(i, late):
        other = (4 * i + part + (1 if late else 31)) % 32
        u = 1 if late else 0
        return remote(
            edge.at[i, u], eb.at[1 - u, plane], e_s.at[u, i], e_r.at[1 - u, plane], {"ctx": other}
        )

    e_arrival = lambda h, s: remote(edge.at[0, 0], eb.at[s, h], e_s.at[0, 0], e_r.at[s, h], partner)
    loop(1, 8, lambda d: a_copy(d).start())

    def edge_start(i):
        e_copy(i, True).start()
        e_copy(i, False).start()

    loop(0, 8, edge_start)
    at_in[plane] = att[plane]
    for c in halos:
        c.wait()
    ge[0:8] = halo[1, 0].astype(F32)
    ge[136:144] = halo[1, 1].astype(F32)
    loop(1, 8, lambda d: q_copy(d).wait_send())
    loop(1, 32, lambda d: kv_copy(d).wait_send())
    loop(1, 8, lambda d: a_copy(d).wait())

    def edge_wait(i):
        e_copy(i, True).wait_send()
        e_copy(i, False).wait_send()
        e_arrival(i, 0).wait_recv()
        e_arrival(i, 1).wait_recv()

    loop(0, 8, edge_wait)

    am[...] = at_in[...].astype(F32).reshape(H * E, T).T.astype(BF)
    pair = lambda src, dst, n: remote(src, dst, p_s.at[n], p_r.at[n], partner)
    send_att = pair(am, ap, 0)
    send_att.start()
    sides = jnp.concatenate(
        [jnp.concatenate([eb[s, h][:, :E] for h in range(H)], axis=1) for s in range(2)], axis=0
    )

    def chunk(c):
        cols = pl.ds(pl.multiple_of(c * 128, 128), 128)
        wc = w_ref[cols, :]
        main = lax.dot_general(am[...], wc, NT, preferred_element_type=F32)
        rim = lax.dot_general(sides, wc, NT, preferred_element_type=F32)
        rnd = lambda y: y.astype(BF).astype(F32)
        mx[8:136] = rnd(x_ref[:, cols].astype(F32) + main)
        mx[0:8] = rnd(halo[0, 0, :, cols].astype(F32) + rim[0:8])
        mx[136:144] = rnd(halo[0, 1, :, cols].astype(F32) + rim[8:16])
        conv = jnp.zeros((136, 128), F32)
        for j in range(9):
            conv = conv + mx[pl.ds(j, 136)] * mk[j] * cf[j : j + 1, cols]
        gate = jax.nn.sigmoid(conv)
        cg = ge[pl.ds(4, 136), cols] * gate * (1.0 + conv * (1.0 - gate))
        cs[...] = rnd(cg)
        silu = conv * gate
        lo_ref[:, cols] = (mx[8:136] + silu[4:132]).astype(BF)
        deep = ge[8:136, cols]
        for j in range(9):
            deep = deep + cs[pl.ds(8 - j, 128)] * mk[8 - j, pl.ds(4, 128)] * cf[j : j + 1, cols]
        ig = deep.astype(BF)
        ig_ref[:, cols] = ig
        igs[c // 2, :, pl.ds(pl.multiple_of((c % 2) * 128, 128), 128)] = ig
        cg_own = cs[pl.ds(4, 128)]
        sums = []
        for j in range(9):
            sums.append(
                jnp.sum(cg_own * mx[pl.ds(4 + j, 128)] * mk[j, pl.ds(4, 128)], axis=0, keepdims=True)
            )
        sums.append(jnp.zeros((7, 128), F32))
        kg[c] = jnp.concatenate(sums, axis=0)

    loop(0, 8, chunk)
    send_ig = [pair(igs.at[2 * z + 1 - core], igp.at[z], 1 + z) for z in range(2)]
    for c in send_ig:
        c.start()
    ag = jnp.zeros((T, H * E), F32)
    for z in range(4):
        ag = ag + jnp.dot(igs[z], w_ref[z * 256 : (z + 1) * 256, :], preferred_element_type=F32)
    dos[...] = ag.astype(BF).astype(F32).T.astype(BF).reshape(H, E, T)
    d_copy = lambda d: remote(dos.at[(plane + d) % 8], do_in.at[plane], d_s.at[d], d_r.at[d], plane_at(d))
    loop(1, 8, lambda d: d_copy(d).start())
    do_in[plane] = dos[plane]

    k1_copy = lambda d: remote(kg.at[(plane + d) % 8], k1.at[plane], k1_s.at[d], k1_r.at[d], plane_at(d))
    k2_copy = lambda d: remote(ksum.at[0], k2.at[dp * 4 + part], k2_s.at[d], k2_r.at[d], column_at(d))
    k3_copy = lambda d: remote(ksum.at[1], kall.at[plane], k3_s.at[d], k3_r.at[d], plane_at(d))
    loop(1, 8, lambda d: k1_copy(d).start())
    k1[plane] = kg[plane]

    w_copy = lambda d: remote(wg.at[(chip + d) % 64], wg_in.at[d], w_s.at[d], w_r.at[d], chip_at(d))
    send_att.wait()
    for c in send_ig:
        c.wait()
    for z in range(2):
        part_sum = lax.dot_general(igs[2 * z + core], am[...], TN, preferred_element_type=F32)
        part_sum = part_sum + lax.dot_general(igp[z], ap[...], TN, preferred_element_type=F32)
        wg[z * 32 : (z + 1) * 32] = part_sum.reshape(32, 8, H * E).astype(BF)
    loop(1, 64, lambda d: w_copy(d).start())

    dqa[...] = jnp.zeros((H, E, T), F32)
    zero = jnp.zeros((E, T), BF)
    loop(1, 8, lambda d: d_copy(d).wait())
    for i in range(H):
        dot = do_in[i]
        rows[i] = jnp.sum(dot.astype(F32) * att[i].astype(F32), axis=0, keepdims=True)
        both[i, E : 2 * E, T:] = dot
        pair_t = jnp.concatenate(
            [
                jnp.concatenate([both[i, :E, :T], zero], axis=0),
                jnp.concatenate([zero, dot], axis=0),
            ],
            axis=1,
        )
        back[i * 2 * T : (i + 1) * 2 * T] = pair_t.astype(F32).T.astype(BF)
    loop(1, 8, lambda d: k1_copy(d).wait())
    ksum[0] = jnp.sum(k1[...], axis=0)
    k2[dp * 4 + part] = ksum[0]
    loop(1, 16, lambda d: k2_copy(d).start())

    g_copy = lambda d: remote(
        dks.at[d], dkv_in.at[d], g_s.at[d], g_r.at[d], {"ctx": (me - d + 32) % 32}
    )

    def backward_step(t):
        for i in range(H):
            sd = jnp.dot(kx[t], both[i], preferred_element_type=F32)
            p = jnp.exp(sd[:, :T] - lse[i])
            ds = (p * (sd[:, T:] - rows[i])).astype(BF)
            dsp[:, i * 2 * T : i * 2 * T + T] = ds
            dsp[:, i * 2 * T + T : (i + 1) * 2 * T] = p.astype(BF)
            dqa[i] += jnp.dot(kt[t, :E], ds, preferred_element_type=F32)
        dkv = jnp.dot(dsp[...], back[...], preferred_element_type=F32).astype(BF)
        dks[2 * t] = dkv[:T]
        dks[2 * t + 1] = dkv[T:]

        @pl.when(t > 0)
        def _():
            g_copy(2 * t).start()

        g_copy(2 * t + 1).start()

    loop(0, NB // 2, backward_step)
    loop(1, 16, lambda d: k2_copy(d).wait())
    ksum[1] = jnp.sum(k2[...], axis=0)
    kall[plane] = ksum[1]
    loop(1, 8, lambda d: k3_copy(d).start())
    loop(NB // 2, NB, backward_step)
    for i in range(H):
        dqs[i] = dqa[i].astype(BF)
    y_copy = lambda d: remote(dqs.at[(plane + d) % 8], dq_in.at[plane], y_s.at[d], y_r.at[d], plane_at(d))
    loop(1, 8, lambda d: y_copy(d).start())
    dq_in[plane] = dqs[plane]
    dkv_in[0] = dks[0]

    loop(1, 8, lambda d: k3_copy(d).wait())
    ko_ref[...] = kall[...]

    def add(d, total):
        w_copy(d).wait()
        return total + wg_in[d].astype(F32)

    wo_ref[...] = lax.fori_loop(1, 64, add, wg[chip].astype(F32))
    loop(1, 8, lambda d: y_copy(d).wait())
    dq_ref[...] = (dq_in[...].astype(F32).reshape(H * E, T) * SCALE).T.astype(BF)
    loop(1, 32, lambda d: g_copy(d).wait())
    for h in range(H):
        parts = [dkv_in[(4 * h + p - me + 32) % 32].astype(F32) for p in range(4)]
        total = (parts[0] + parts[1]) + (parts[2] + parts[3])
        cols = slice(h * E, (h + 1) * E)
        dk_ref[:, cols] = total[:, :E].astype(BF)
        dv_ref[:, cols] = total[:, E:].astype(BF)


def layer(lens, q, k, v, x, g, w, ck):
    dma = pltpu.SemaphoreType.DMA
    V = pltpu.VMEM
    return pl.pallas_call(
        layer_kernel,
        name="layer",
        out_shape=(
            jax.ShapeDtypeStruct((T, C), BF),
            jax.ShapeDtypeStruct((T, C), BF),
            jax.ShapeDtypeStruct((T, H * E), BF),
            jax.ShapeDtypeStruct((T, H * E), BF),
            jax.ShapeDtypeStruct((T, H * E), BF),
            jax.ShapeDtypeStruct((8, H * E), F32),
            jax.ShapeDtypeStruct((8, 16, 128), F32),
        ),
        in_specs=[pl.BlockSpec(memory_space=pltpu.SMEM)] + vm(7),
        out_specs=tuple(vm(7)),
        scratch_shapes=[
            V((H, T, 2 * E), BF),
            V((H, E, T), BF),
            V((32, T, 2 * E), BF),
            V((H, E, T), BF),
            V((2, 2, 8, C), BF),
            V((NB, KB, 4 * E), BF),
            V((NB, 2 * E, KB), BF),
            V((H, 4 * E, 2 * T), BF),
            V((H * 2 * T, 2 * E), BF),
            V((H, 1, T), F32),
            V((H, 8, T), F32),
            V((H, E, T), F32),
            V((H, 1, T), F32),
            V((H, 1, T), F32),
            V((H, E, T), BF),
            V((H, 2, 8, 128), BF),
            V((H, E, T), BF),
            V((2, H, 8, 128), BF),
            V((T, H * E), BF),
            V((T, H * E), BF),
            V((4, T, 256), BF),
            V((2, T, 256), BF),
            V((H, E, T), BF),
            V((H, E, T), BF),
            V((144, 128), F32),
            V((144, C), F32),
            V((136, 128), F32),
            V((9, 136, 128), F32),
            V((16, C), F32),
            V((64, 8, H * E), BF),
            V((64, 8, H * E), BF),
            V((8, 16, 128), F32),
            V((8, 16, 128), F32),
            V((16, 16, 128), F32),
            V((2, 16, 128), F32),
            V((8, 16, 128), F32),
            V((KB, H * 2 * T), BF),
            V((H, E, T), F32),
            V((32, T, 2 * E), BF),
            V((32, T, 2 * E), BF),
            V((H, E, T), BF),
            V((H, E, T), BF),
        ]
        + [dma((n,)) for n in (32, 32, 8, 8)]
        + [dma((2, 2))] * 2
        + [dma((8,))] * 2
        + [dma((2, 8))] * 2
        + [dma((n,)) for n in (8, 8, 3, 3, 64, 64, 8, 8, 16, 16, 8, 8, 32, 32, 8, 8)],
        compiler_params=pltpu.CompilerParams(collective_id=0, has_side_effects=True),
    )(lens, q, k, v, x, g, w, ck)


def hand_on_kernel(a, b, c, d, e, f, k, ao, bo, co, do, eo, fo, ko):
    for src, dst in ((a, ao), (b, bo), (c, co), (d, do), (e, eo), (f, fo)):
        dst[...] = src[...]
    for h in range(8):
        ko[:, h * 128 : (h + 1) * 128] = k[h, :9]


def hand_on(*xs):
    shapes = [jax.ShapeDtypeStruct(x.shape, x.dtype) for x in xs[:6]]
    return pl.pallas_call(
        hand_on_kernel,
        name="hand_on",
        out_shape=tuple(shapes) + (jax.ShapeDtypeStruct((9, C), F32),),
        in_specs=vm(7),
        out_specs=tuple(vm(7)),
    )(*xs)


def body(x, q, k, v, w, ck, lens, g):
    outs = hand_on(*layer(lens, q, k, v, x, g, w, ck.T))
    return outs[:6] + (outs[6].T,)


def solution(mesh):
    row = P(("dp", "ctx"), None)
    return jax.shard_map(
        body,
        mesh=mesh,
        in_specs=(row, row, row, row, P(), P(), P(), row),
        out_specs=(row, row, row, row, row, row, P()),
        check_vma=False,
    )
```

time: 1300 us -> 120 us (0.09)
  the two profiles are of different devices: /device:TPU:96 before, /device:TPU:1 now
where the time goes in v4:
time: 120 us; the launch traced here: 118 us
  Pallas kernels  117 us (98%)
    pallas_call x1, Pallas kernels, layer(): pl.pallas_call(layer_kernel, name='layer', out_shape=(jax.ShapeDtypeStruc...  115 us

profile of v4, /device:TPU:1, one launch (start us, length us, event | category | flops | bytes accessed | tf_op | source)
XLA Modules:
  0.0 118.0 jit_solution(2307264044159275312)
XLA Ops:
  0.6 115.2 %layer.1 = (bf16[128,1024]{1,0:T(8,128)(2,1)}, bf16[128,1024]{1,0:T(8,128)(2,1)}, bf16[128,512]{1,0:T(8,128)(2,1)}, bf16[128,512]{1,0:T(8,128)(2,1)}, bf16[128,5...) custom-call(s32[4,4]{1,0:T(4,128)} %len_ref.1, bf16[128,512]{1,0:T(8,128)(2,1)} %q_ref.1, ...), custom_call_target="tpu_custom_call" | custom-call | tf_op jit(solution)/shard_map/layer/pallas_call | solution.py:362
  115.8 2.1 %hand_on.1 = (bf16[128,1024]{1,0:T(8,128)(2,1)}, bf16[128,1024]{1,0:T(8,128)(2,1)}, bf16[128,512]{1,0:T(8,128)(2,1)}, bf16[128,512]{1,0:T(8,128)(2,1)}, bf16[128...) custom-call(bf16[128,1024]{1,0:T(8,128)(2,1)} %get-tuple-element.21.a, ...), custom_call_target="tpu_custom_call" | custom-call | tf_op jit(solution)/shard_map/hand_on/pallas_call | solution.py:438

commit v5 on v4

--- a/solution.py
+++ b/solution.py
@@ -47,7 +47,7 @@
     lo_ref, ig_ref, dq_ref, dk_ref, dv_ref, wo_ref, ko_ref,
     kvs, qs, kv_in, q_in, halo, kx, kt, both, back, m1, l8, acc, lse, rows, att, edge,
     at_in, eb, am, ap, igs, igp, dos, do_in, mx, ge, cs, mk, cf, wg, wg_in,
-    kg, k1, k2, ksum, kall, dsp, dqa, dks, dkv_in, dqs, dq_in,
+    kg, k1, k2, ksum, kall, st_a, st_b, sd_a, sd_b, pt_a, pt_b, ds_a, ds_b, top, dqa, dks, dkv_in, dqs, dq_in,
     kv_s, kv_r, q_s, q_r, h_s, h_r, a_s, a_r, e_s, e_r, d_s, d_r, p_s, p_r,
     w_s, w_r, k1_s, k1_r, k2_s, k2_r, k3_s, k3_r, g_s, g_r, y_s, y_r,
 ):
@@ -116,9 +116,9 @@
     for c in halos:
         c.start()
 
-    m1[...] = jnp.full((H, 1, T), NEG, F32)
-    l8[...] = jnp.zeros((H, 8, T), F32)
-    acc[...] = jnp.zeros((H, E, T), F32)
+    m1[...] = jnp.full((1, H * T), NEG, F32)
+    l8[...] = jnp.zeros((8, H * T), F32)
+    acc[...] = jnp.zeros((E, H * T), F32)
     lane = lax.broadcasted_iota(jnp.int32, (1, 2 * E), 1)
     pick = lambda a, b, c, d, e: jnp.where(
         lane == 0, a, jnp.where(lane == 1, b, jnp.where(lane == 2, c, jnp.where(lane == 3, d, e)))
@@ -144,37 +144,70 @@
     for i in range(H):
         both[i, :E, :T] = q_in[(plane - i + 8) % 8]
 
-    def arrive(d):
-        kv_copy(d).wait_recv()
-
-    def forward_step(t):
-        @pl.when(t > 0)
-        def _():
-            arrive(2 * t)
-
-        arrive(2 * t + 1)
+    def build(t):
         for u in range(2):
             kv = kv_in[2 * t + u]
-            kt[t, :, u * T : (u + 1) * T] = kv.astype(F32).T.astype(BF)
             at = slice(u * T, (u + 1) * T)
+            kt[t, :, at] = kv.astype(F32).T.astype(BF)
             kx[t, at, : 2 * E] = kv
             p = (me - 2 * t - u + 32) % 32 * T + lax.broadcasted_iota(jnp.int32, (T, 2 * E), 0)
             kx[t, at, 2 * E :] = jnp.where((p >= begin) & (p < end), 1.0, 0.0).astype(BF)
+
+    def score(t, st):
         for i in range(H):
             s = jnp.dot(kx[t], both[i, :, :T], preferred_element_type=F32)
-            old = m1[i]
-            new = jnp.maximum(old, jnp.max(fold(s, jnp.max), axis=0, keepdims=True))
-            p = jnp.exp(s - new)
-            scale = jnp.exp(old - new)
-            m1[i] = new
-            l8[i] = l8[i] * scale + fold(p, jnp.sum)
-            acc[i] = acc[i] * scale + jnp.dot(kt[t, E:], p.astype(BF), preferred_element_type=F32)
-
-    loop(0, NB, forward_step)
+            st[i] = s
+            top[:, i * T : (i + 1) * T] = fold(s, jnp.max)
+
+    def weigh(t, st, pt):
+        old = m1[...]
+        new = jnp.maximum(old, jnp.max(top[...], axis=0, keepdims=True))
+        scale = jnp.exp(old - new)
+        m1[...] = new
+        return new, scale
+
+    def spread(t, st, pt, new, scale):
+        for i in range(H):
+            cols = slice(i * T, (i + 1) * T)
+            p = jnp.exp(st[i] - new[:, cols])
+            l8[:, cols] = l8[:, cols] * scale[:, cols] + fold(p, jnp.sum)
+            pt[:, cols] = p.astype(BF)
+        for i in range(0, H, 2):
+            cols = slice(i * T, (i + 2) * T)
+            acc[:, cols] = acc[:, cols] * scale[:, cols] + jnp.dot(
+                kt[t, E:], pt[:, cols], preferred_element_type=F32
+            )
+
+    kv_copy(1).wait_recv()
+    build(0)
+    score(0, st_a)
+
+    def forward_step(u):
+        t = 2 * u
+        kv_copy(2 * t + 2).wait_recv()
+        kv_copy(2 * t + 3).wait_recv()
+
+        @pl.when(u < NB // 2 - 1)
+        def _():
+            kv_copy(2 * t + 4).wait_recv()
+            kv_copy(2 * t + 5).wait_recv()
+
+        later = jnp.minimum(t + 2, NB - 1)
+        build(t + 1)
+        build(later)
+        w = weigh(t, st_a, pt_a)
+        score(t + 1, st_b)
+        spread(t, st_a, pt_a, *w)
+        w = weigh(t + 1, st_b, pt_b)
+        score(later, st_a)
+        spread(t + 1, st_b, pt_b, *w)
+
+    loop(0, NB // 2, forward_step)
     for i in range(H):
-        total = jnp.sum(l8[i], axis=0, keepdims=True)
-        lse[i] = m1[i] + jnp.log(total)
-        out = acc[i] / total
+        cols = slice(i * T, (i + 1) * T)
+        total = jnp.sum(l8[:, cols], axis=0, keepdims=True)
+        lse[:, cols] = m1[:, cols] + jnp.log(total)
+        out = acc[:, cols] / total
         att[i] = out.astype(BF)
         wide = jnp.concatenate([out, jnp.zeros((E, T), F32)], axis=0).T
         edge[i, 0] = wide[:8].astype(BF)
@@ -282,7 +315,7 @@
         wg[z * 32 : (z + 1) * 32] = part_sum.reshape(32, 8, H * E).astype(BF)
     loop(1, 64, lambda d: w_copy(d).start())
 
-    dqa[...] = jnp.zeros((H, E, T), F32)
+    dqa[...] = jnp.zeros((E, H * T), F32)
     zero = jnp.zeros((E, T), BF)
     loop(1, 8, lambda d: d_copy(d).wait())
     for i in range(H):
@@ -296,7 +329,9 @@
             ],
             axis=1,
         )
-        back[i * 2 * T : (i + 1) * 2 * T] = pair_t.astype(F32).T.astype(BF)
+        turned = pair_t.astype(F32).T.astype(BF)
+        back[i * T : (i + 1) * T] = turned[:T]
+        back[(H + i) * T : (H + i + 1) * T] = turned[T:]
     loop(1, 8, lambda d: k1_copy(d).wait())
     ksum[0] = jnp.sum(k1[...], axis=0)
     k2[dp * 4 + part] = ksum[0]
@@ -306,32 +341,50 @@
         dks.at[d], dkv_in.at[d], g_s.at[d], g_r.at[d], {"ctx": (me - d + 32) % 32}
     )
 
-    def backward_step(t):
+    def product(t, sd):
         for i in range(H):
-            sd = jnp.dot(kx[t], both[i], preferred_element_type=F32)
-            p = jnp.exp(sd[:, :T] - lse[i])
-            ds = (p * (sd[:, T:] - rows[i])).astype(BF)
-            dsp[:, i * 2 * T : i * 2 * T + T] = ds
-            dsp[:, i * 2 * T + T : (i + 1) * 2 * T] = p.astype(BF)
-            dqa[i] += jnp.dot(kt[t, :E], ds, preferred_element_type=F32)
-        dkv = jnp.dot(dsp[...], back[...], preferred_element_type=F32).astype(BF)
+            sd[i] = jnp.dot(kx[t], both[i], preferred_element_type=F32)
+
+    def backward_part(t, sd, pt, dst):
+        for i in range(H):
+            cols = slice(i * T, (i + 1) * T)
+            p = jnp.exp(sd[i, :, :T] - lse[:, cols])
+            ds = (p * (sd[i, :, T:] - rows[i])).astype(BF)
+            dst[:, cols] = ds
+            pt[:, cols] = p.astype(BF)
+        for i in range(0, H, 2):
+            cols = slice(i * T, (i + 2) * T)
+            dqa[:, cols] += jnp.dot(kt[t, :E], dst[:, cols], preferred_element_type=F32)
+        dkv = jnp.dot(dst[...], back[: H * T], preferred_element_type=F32)
+        dkv = dkv + jnp.dot(pt[...], back[H * T :], preferred_element_type=F32)
+        dkv = dkv.astype(BF)
         dks[2 * t] = dkv[:T]
         dks[2 * t + 1] = dkv[T:]
 
-        @pl.when(t > 0)
+    def backward_step(u):
+        t = 2 * u
+        product(t + 1, sd_b)
+        backward_part(t, sd_a, pt_a, ds_a)
+        product(jnp.minimum(t + 2, NB - 1), sd_a)
+        backward_part(t + 1, sd_b, pt_b, ds_b)
+
+        @pl.when(u > 0)
         def _():
             g_copy(2 * t).start()
 
         g_copy(2 * t + 1).start()
-
-    loop(0, NB // 2, backward_step)
+        g_copy(2 * t + 2).start()
+        g_copy(2 * t + 3).start()
+
+    product(0, sd_a)
+    loop(0, NB // 4, backward_step)
     loop(1, 16, lambda d: k2_copy(d).wait())
     ksum[1] = jnp.sum(k2[...], axis=0)
     kall[plane] = ksum[1]
     loop(1, 8, lambda d: k3_copy(d).start())
-    loop(NB // 2, NB, backward_step)
+    loop(NB // 4, NB // 2, backward_step)
     for i in range(H):
-        dqs[i] = dqa[i].astype(BF)
+        dqs[i] = dqa[:, i * T : (i + 1) * T].astype(BF)
     y_copy = lambda d: remote(dqs.at[(plane + d) % 8], dq_in.at[plane], y_s.at[d], y_r.at[d], plane_at(d))
     loop(1, 8, lambda d: y_copy(d).start())
     dq_in[plane] = dqs[plane]
@@ -383,10 +436,10 @@
             V((NB, 2 * E, KB), BF),
             V((H, 4 * E, 2 * T), BF),
             V((H * 2 * T, 2 * E), BF),
-            V((H, 1, T), F32),
-            V((H, 8, T), F32),
-            V((H, E, T), F32),
-            V((H, 1, T), F32),
+            V((1, H * T), F32),
+            V((8, H * T), F32),
+            V((E, H * T), F32),
+            V((1, H * T), F32),
             V((H, 1, T), F32),
             V((H, E, T), BF),
             V((H, 2, 8, 128), BF),
@@ -410,8 +463,16 @@
             V((16, 16, 128), F32),
             V((2, 16, 128), F32),
             V((8, 16, 128), F32),
-            V((KB, H * 2 * T), BF),
-            V((H, E, T), F32),
+            V((H, KB, T), F32),
+            V((H, KB, T), F32),
+            V((H, KB, 2 * T), F32),
+            V((H, KB, 2 * T), F32),
+            V((KB, H * T), BF),
+            V((KB, H * T), BF),
+            V((KB, H * T), BF),
+            V((KB, H * T), BF),
+            V((8, H * T), F32),
+            V((E, H * T), F32),
             V((32, T, 2 * E), BF),
             V((32, T, 2 * E), BF),
             V((H, E, T), BF),

time: 120 us -> 95.1 us (0.79); the launches traced: 118 us -> 94.7 us
  Pallas kernels: 117 us -> 94.1 us
    pallas_call x1, Pallas kernels: 115 us -> 92 us  [layer(): pl.pallas_call(layer_kernel, name='layer', out_shape=(jax.ShapeDtypeStruc...]
where the time goes in v5:
time: 95.1 us; the launch traced here: 94.7 us
  Pallas kernels  94.1 us (99%)
    pallas_call x1, Pallas kernels, layer(): pl.pallas_call(layer_kernel, name='layer', out_shape=(jax.ShapeDtypeStruc...  92 us
    pallas_call x1, Pallas kernels, hand_on(): pl.pallas_call(hand_on_kernel, name='hand_on', out_shape=tuple(shapes) +...  2.14 us

profile of v5, /device:TPU:1, one launch (start us, length us, event | category | flops | bytes accessed | tf_op | source)
XLA Modules:
  0.0 94.7 jit_solution(17992237536317850351)
XLA Ops:
  0.6 92.0 %layer.1 = (bf16[128,1024]{1,0:T(8,128)(2,1)}, bf16[128,1024]{1,0:T(8,128)(2,1)}, bf16[128,512]{1,0:T(8,128)(2,1)}, bf16[128,512]{1,0:T(8,128)(2,1)}, bf16[128,5...) custom-call(s32[4,4]{1,0:T(4,128)} %len_ref.1, bf16[128,512]{1,0:T(8,128)(2,1)} %q_ref.1, ...), custom_call_target="tpu_custom_call" | custom-call | tf_op jit(solution)/shard_map/layer/pallas_call | solution.py:415
  92.6 2.1 %hand_on.1 = (bf16[128,1024]{1,0:T(8,128)(2,1)}, bf16[128,1024]{1,0:T(8,128)(2,1)}, bf16[128,512]{1,0:T(8,128)(2,1)}, bf16[128,512]{1,0:T(8,128)(2,1)}, bf16[128...) custom-call(bf16[128,1024]{1,0:T(8,128)(2,1)} %get-tuple-element.21.a, ...), custom_call_target="tpu_custom_call" | custom-call | tf_op jit(solution)/shard_map/hand_on/pallas_call | solution.py:499

commit v6 on v5

--- a/solution.py
+++ b/solution.py
@@ -49,7 +49,7 @@
     at_in, eb, am, ap, igs, igp, dos, do_in, mx, ge, cs, mk, cf, wg, wg_in,
     kg, k1, k2, ksum, kall, st_a, st_b, sd_a, sd_b, pt_a, pt_b, ds_a, ds_b, top, dqa, dks, dkv_in, dqs, dq_in,
     kv_s, kv_r, q_s, q_r, h_s, h_r, a_s, a_r, e_s, e_r, d_s, d_r, p_s, p_r,
-    w_s, w_r, k1_s, k1_r, k2_s, k2_r, k3_s, k3_r, g_s, g_r, y_s, y_r,
+    f_s, f_r, r_s, r_r, w_s, w_r, k1_s, k1_r, k2_s, k2_r, k3_s, k3_r, g_s, g_r, y_s, y_r,
 ):
     dp, me = lax.axis_index("dp"), lax.axis_index("ctx")
     core, part, plane = dp % 2, me % 4, me // 4
@@ -96,9 +96,44 @@
     pl.semaphore_wait(barrier, 71)
 
     q_copy = lambda d: remote(qs.at[(plane + d) % 8], q_in.at[d], q_s.at[d], q_r.at[d], plane_at(d))
-    kv_copy = lambda d: remote(
-        kvs.at[((me + d) % 32) // 4], kv_in.at[d], kv_s.at[d], kv_r.at[d], {"ctx": (me + d) % 32}
+    slot = lambda e, f: f // 2 * 16 + 2 * e + f % 2
+    owner = lambda n: (plane - n // 2 % 8 + 8) % 8 * 4 + (part - n // 16 * 2 - n % 2 + 4) % 4
+    kv_copy = lambda e: remote(
+        kvs.at[(plane + e) % 8], kv_in.at[slot(e, 0)], kv_s.at[e], kv_r.at[e], plane_at(e)
     )
+    up, down = {"ctx": plane * 4 + (part + 1) % 4}, {"ctx": plane * 4 + (part + 3) % 4}
+
+    def pass_on(e, n):
+        return remote(
+            kv_in.at[slot(e, 0)], kv_in.at[slot(e, (3, 1)[n])], f_s.at[n, e], f_r.at[n, e], (down, up)[n]
+        )
+
+    def relay(e, n):
+        half = pl.ds((1 - n) * 64, 64)
+        return remote(
+            kv_in.at[slot(e, (3, 1)[n]), half],
+            kv_in.at[slot(e, 2), half],
+            r_s.at[n, e],
+            r_r.at[n, e],
+            (down, up)[n],
+        )
+
+    def stage_pass(e):
+        pass_on(e, 0).start()
+        pass_on(e, 1).start()
+
+    def stage_relay(e):
+        for n in range(2):
+            pass_on(e, n).wait_recv()
+            relay(e, n).start()
+
+    def stage_last(e):
+        relay(e, 0).wait_recv()
+        relay(e, 1).wait_recv()
+
+    def stage_first(e):
+        kv_copy(e).wait_recv()
+        stage_pass(e)
 
     def halo_copy(a, up):
         ref, s = (x_ref, g_ref)[a], 0 if up else 1
@@ -112,7 +147,8 @@
 
     halos = [halo_copy(a, up) for a in range(2) for up in (True, False)]
     loop(1, 8, lambda d: q_copy(d).start())
-    loop(1, 32, lambda d: kv_copy(d).start())
+    loop(1, 8, lambda e: kv_copy(e).start())
+    stage_pass(0)
     for c in halos:
         c.start()
 
@@ -150,7 +186,7 @@
             at = slice(u * T, (u + 1) * T)
             kt[t, :, at] = kv.astype(F32).T.astype(BF)
             kx[t, at, : 2 * E] = kv
-            p = (me - 2 * t - u + 32) % 32 * T + lax.broadcasted_iota(jnp.int32, (T, 2 * E), 0)
+            p = owner(2 * t + u) * T + lax.broadcasted_iota(jnp.int32, (T, 2 * E), 0)
             kx[t, at, 2 * E :] = jnp.where((p >= begin) & (p < end), 1.0, 0.0).astype(BF)
 
     def score(t, st):
@@ -178,19 +214,29 @@
                 kt[t, E:], pt[:, cols], preferred_element_type=F32
             )
 
-    kv_copy(1).wait_recv()
+    loop(1, 8, stage_first)
+    stage_relay(0)
     build(0)
     score(0, st_a)
 
     def forward_step(u):
         t = 2 * u
-        kv_copy(2 * t + 2).wait_recv()
-        kv_copy(2 * t + 3).wait_recv()
-
-        @pl.when(u < NB // 2 - 1)
+
+        @pl.when(u < 4)
         def _():
-            kv_copy(2 * t + 4).wait_recv()
-            kv_copy(2 * t + 5).wait_recv()
+            stage_relay(2 * u + 1)
+
+        @pl.when(u < 3)
+        def _():
+            stage_relay(2 * u + 2)
+
+        @pl.when(u > 3)
+        def _():
+            stage_last(2 * u - 7)
+
+        @pl.when((u > 2) & (u < 7))
+        def _():
+            stage_last(2 * u - 6)
 
         later = jnp.minimum(t + 2, NB - 1)
         build(t + 1)
@@ -236,7 +282,14 @@
     ge[0:8] = halo[1, 0].astype(F32)
     ge[136:144] = halo[1, 1].astype(F32)
     loop(1, 8, lambda d: q_copy(d).wait_send())
-    loop(1, 32, lambda d: kv_copy(d).wait_send())
+    loop(1, 8, lambda e: kv_copy(e).wait_send())
+
+    def sent(e):
+        for n in range(2):
+            pass_on(e, n).wait_send()
+            relay(e, n).wait_send()
+
+    loop(0, 8, sent)
     loop(1, 8, lambda d: a_copy(d).wait())
 
     def edge_wait(i):
@@ -337,8 +390,12 @@
     k2[dp * 4 + part] = ksum[0]
     loop(1, 16, lambda d: k2_copy(d).start())
 
-    g_copy = lambda d: remote(
-        dks.at[d], dkv_in.at[d], g_s.at[d], g_r.at[d], {"ctx": (me - d + 32) % 32}
+    g_copy = lambda n: remote(
+        dks.at[n],
+        dkv_in.at[n],
+        g_s.at[n],
+        g_r.at[n],
+        {"ctx": owner(n)},
     )
 
     def product(t, sd):
@@ -402,7 +459,7 @@
     dq_ref[...] = (dq_in[...].astype(F32).reshape(H * E, T) * SCALE).T.astype(BF)
     loop(1, 32, lambda d: g_copy(d).wait())
     for h in range(H):
-        parts = [dkv_in[(4 * h + p - me + 32) % 32].astype(F32) for p in range(4)]
+        parts = [dkv_in[slot((h - plane + 8) % 8, f)].astype(F32) for f in range(4)]
         total = (parts[0] + parts[1]) + (parts[2] + parts[3])
         cols = slice(h * E, (h + 1) * E)
         dk_ref[:, cols] = total[:, :E].astype(BF)
@@ -478,11 +535,13 @@
             V((H, E, T), BF),
             V((H, E, T), BF),
         ]
-        + [dma((n,)) for n in (32, 32, 8, 8)]
+        + [dma((n,)) for n in (8, 8, 8, 8)]
         + [dma((2, 2))] * 2
         + [dma((8,))] * 2
         + [dma((2, 8))] * 2
-        + [dma((n,)) for n in (8, 8, 3, 3, 64, 64, 8, 8, 16, 16, 8, 8, 32, 32, 8, 8)],
+        + [dma((n,)) for n in (8, 8, 3, 3)]
+        + [dma((2, 8))] * 4
+        + [dma((n,)) for n in (64, 64, 8, 8, 16, 16, 8, 8, 32, 32, 8, 8)],
         compiler_params=pltpu.CompilerParams(collective_id=0, has_side_effects=True),
     )(lens, q, k, v, x, g, w, ck)
 

time: 95.1 us -> 83.9 us (0.88)
  Pallas kernels: 94.1 us -> 83.1 us
    pallas_call x1, Pallas kernels: 92 us -> 80.9 us  [layer(): pl.pallas_call(layer_kernel, name='layer', out_shape=(jax.ShapeDtypeStruc...]
where the time goes in v6:
time: 83.9 us; the launch traced here: 83.7 us
  Pallas kernels  83.1 us (99%)
    pallas_call x1, Pallas kernels, layer(): pl.pallas_call(layer_kernel, name='layer', out_shape=(jax.ShapeDtypeStruc...  80.9 us
    pallas_call x1, Pallas kernels, hand_on(): pl.pallas_call(hand_on_kernel, name='hand_on', out_shape=tuple(shapes) +...  2.14 us

profile of v6, /device:TPU:1, one launch (start us, length us, event | category | flops | bytes accessed | tf_op | source)
XLA Modules:
  0.0 83.7 jit_solution(15429933030892039336)
XLA Ops:
  0.6 80.9 %layer.1 = (bf16[128,1024]{1,0:T(8,128)(2,1)}, bf16[128,1024]{1,0:T(8,128)(2,1)}, bf16[128,512]{1,0:T(8,128)(2,1)}, bf16[128,512]{1,0:T(8,128)(2,1)}, bf16[128,5...) custom-call(s32[4,4]{1,0:T(4,128)} %len_ref.1, bf16[128,512]{1,0:T(8,128)(2,1)} %q_ref.1, ...), custom_call_target="tpu_custom_call" | custom-call | tf_op jit(solution)/shard_map/layer/pallas_call | solution.py:472
  81.6 2.1 %hand_on.1 = (bf16[128,1024]{1,0:T(8,128)(2,1)}, bf16[128,1024]{1,0:T(8,128)(2,1)}, bf16[128,512]{1,0:T(8,128)(2,1)}, bf16[128,512]{1,0:T(8,128)(2,1)}, bf16[128...) custom-call(bf16[128,1024]{1,0:T(8,128)(2,1)} %get-tuple-element.21.a, ...), custom_call_target="tpu_custom_call" | custom-call | tf_op jit(solution)/shard_map/hand_on/pallas_call | solution.py:558

commit v7 on v6

--- a/solution.py
+++ b/solution.py
@@ -43,9 +43,9 @@
 
 
 def layer_kernel(
-    len_ref, q_ref, k_ref, v_ref, x_ref, g_ref, w_ref, ck_ref,
-    lo_ref, ig_ref, dq_ref, dk_ref, dv_ref, wo_ref, ko_ref,
-    kvs, qs, kv_in, q_in, halo, kx, kt, both, back, m1, l8, acc, lse, rows, att, edge,
+    len_ref, q_hbm, k_hbm, v_hbm, x_hbm, g_hbm, w_hbm, ck_ref,
+    lo_hbm, ig_hbm, dq_ref, dk_ref, dv_ref, wo_ref, ko_ref,
+    q_ref, k_ref, v_ref, x_ref, g_ref, w_ref, lo_ref, ig_ref, load, kvs, qs, kv_in, q_in, halo, kx, kt, both, back, m1, l8, acc, lse, rows, att, edge,
     at_in, eb, am, ap, igs, igp, dos, do_in, mx, ge, cs, mk, cf, wg, wg_in,
     kg, k1, k2, ksum, kall, st_a, st_b, sd_a, sd_b, pt_a, pt_b, ds_a, ds_b, top, dqa, dks, dkv_in, dqs, dq_in,
     kv_s, kv_r, q_s, q_r, h_s, h_r, a_s, a_r, e_s, e_r, d_s, d_r, p_s, p_r,
@@ -67,6 +67,11 @@
         other = (dp * 4 + part + d) % 16
         return {"dp": other // 4, "ctx": plane * 4 + other % 4}
 
+    homes = ((q_hbm, q_ref), (k_hbm, k_ref), (v_hbm, v_ref), (g_hbm, g_ref), (x_hbm, x_ref), (w_hbm, w_ref))
+    loads = [pltpu.make_async_copy(src, dst, load.at[n]) for n, (src, dst) in enumerate(homes)]
+    for c in loads:
+        c.start()
+
     barrier = pltpu.get_barrier_semaphore()
 
     def signal(where):
@@ -75,6 +80,8 @@
     loop(1, 64, lambda d: signal(chip_at(d)))
     loop(0, 8, lambda d: signal({"dp": (d // 4) * 2 + 1 - core, "ctx": plane * 4 + d % 4}))
 
+    for c in loads[:3]:
+        c.wait()
     for h in range(H):
         cols = slice(h * E, (h + 1) * E)
         kvs[h] = jnp.concatenate([k_ref[:, cols], v_ref[:, cols]], axis=1)
@@ -149,6 +156,8 @@
     loop(1, 8, lambda d: q_copy(d).start())
     loop(1, 8, lambda e: kv_copy(e).start())
     stage_pass(0)
+    for c in loads[3:]:
+        c.wait()
     for c in halos:
         c.start()
 
@@ -176,6 +185,13 @@
     cf[0:9] = ck_ref[...].astype(F32)
     ge[8:136] = g_ref[...].astype(F32)
 
+    def mark(t):
+        for u in range(2):
+            p = owner(2 * t + u) * T + lax.broadcasted_iota(jnp.int32, (T, 2 * E), 0)
+            one = jnp.where((p >= begin) & (p < end), 1.0, 0.0).astype(BF)
+            kx[t, u * T : (u + 1) * T, 2 * E :] = one
+
+    loop(0, NB, mark)
     loop(1, 8, lambda d: q_copy(d).wait_recv())
     for i in range(H):
         both[i, :E, :T] = q_in[(plane - i + 8) % 8]
@@ -186,8 +202,6 @@
             at = slice(u * T, (u + 1) * T)
             kt[t, :, at] = kv.astype(F32).T.astype(BF)
             kx[t, at, : 2 * E] = kv
-            p = owner(2 * t + u) * T + lax.broadcasted_iota(jnp.int32, (T, 2 * E), 0)
-            kx[t, at, 2 * E :] = jnp.where((p >= begin) & (p < end), 1.0, 0.0).astype(BF)
 
     def score(t, st):
         for i in range(H):
@@ -341,6 +355,10 @@
         kg[c] = jnp.concatenate(sums, axis=0)
 
     loop(0, 8, chunk)
+    stores = [
+        pltpu.make_async_copy(src, dst, load.at[6 + n])
+        for n, (src, dst) in enumerate(((lo_ref, lo_hbm), (ig_ref, ig_hbm)))
+    ]
     send_ig = [pair(igs.at[2 * z + 1 - core], igp.at[z], 1 + z) for z in range(2)]
     for c in send_ig:
         c.start()
@@ -367,6 +385,8 @@
         part_sum = part_sum + lax.dot_general(igp[z], ap[...], TN, preferred_element_type=F32)
         wg[z * 32 : (z + 1) * 32] = part_sum.reshape(32, 8, H * E).astype(BF)
     loop(1, 64, lambda d: w_copy(d).start())
+    for c in stores:
+        c.start()
 
     dqa[...] = jnp.zeros((E, H * T), F32)
     zero = jnp.zeros((E, T), BF)
@@ -447,6 +467,8 @@
     dq_in[plane] = dqs[plane]
     dkv_in[0] = dks[0]
 
+    for c in stores:
+        c.wait()
     loop(1, 8, lambda d: k3_copy(d).wait())
     ko_ref[...] = kall[...]
 
@@ -481,9 +503,18 @@
             jax.ShapeDtypeStruct((8, H * E), F32),
             jax.ShapeDtypeStruct((8, 16, 128), F32),
         ),
-        in_specs=[pl.BlockSpec(memory_space=pltpu.SMEM)] + vm(7),
-        out_specs=tuple(vm(7)),
+        in_specs=[pl.BlockSpec(memory_space=pltpu.SMEM)] + [pl.BlockSpec(memory_space=pl.ANY)] * 6 + vm(1),
+        out_specs=(pl.BlockSpec(memory_space=pl.ANY),) * 2 + tuple(vm(5)),
         scratch_shapes=[
+            V((T, H * E), BF),
+            V((T, H * E), BF),
+            V((T, H * E), BF),
+            V((T, C), BF),
+            V((T, C), BF),
+            V((C, H * E), BF),
+            V((T, C), BF),
+            V((T, C), BF),
+            dma((8,)),
             V((H, T, 2 * E), BF),
             V((H, E, T), BF),
             V((32, T, 2 * E), BF),

time: 83.9 us -> 82.2 us (0.980)
  Pallas kernels: 83.1 us -> 81.3 us
    pallas_call x1, Pallas kernels: 80.9 us -> 79.2 us  [layer(): pl.pallas_call(layer_kernel, name='layer', out_shape=(jax.ShapeDtypeStruc...]
where the time goes in v7:
time: 82.2 us; the launch traced here: 82 us
  Pallas kernels  81.3 us (99%)
    pallas_call x1, Pallas kernels, layer(): pl.pallas_call(layer_kernel, name='layer', out_shape=(jax.ShapeDtypeStruc...  79.2 us
    pallas_call x1, Pallas kernels, hand_on(): pl.pallas_call(hand_on_kernel, name='hand_on', out_shape=tuple(shapes) +...  2.14 us

profile of v7, /device:TPU:1, one launch (start us, length us, event | category | flops | bytes accessed | tf_op | source)
XLA Modules:
  0.0 82.0 jit_solution(5719813591736826632)
XLA Ops:
  0.6 79.2 %layer.1 = (bf16[128,1024]{1,0:T(8,128)(2,1)}, bf16[128,1024]{1,0:T(8,128)(2,1)}, bf16[128,512]{1,0:T(8,128)(2,1)}, bf16[128,512]{1,0:T(8,128)(2,1)}, bf16[128,5...) custom-call(s32[4,4]{1,0:T(4,128)} %len_ref.1, bf16[128,512]{1,0:T(8,128)(2,1)} %q_hbm.1, ...), custom_call_target="tpu_custom_call" | custom-call | tf_op jit(solution)/shard_map/layer/pallas_call | solution.py:494
  79.8 2.1 %hand_on.1 = (bf16[128,1024]{1,0:T(8,128)(2,1)}, bf16[128,1024]{1,0:T(8,128)(2,1)}, bf16[128,512]{1,0:T(8,128)(2,1)}, bf16[128,512]{1,0:T(8,128)(2,1)}, bf16[128...) custom-call(bf16[128,1024]{1,0:T(8,128)(2,1)} %get-tuple-element.21.a, ...), custom_call_target="tpu_custom_call" | custom-call | tf_op jit(solution)/shard_map/hand_on/pallas_call | solution.py:589

commit v8 on v7

--- a/solution.py
+++ b/solution.py
@@ -48,7 +48,7 @@
     q_ref, k_ref, v_ref, x_ref, g_ref, w_ref, lo_ref, ig_ref, load, kvs, qs, kv_in, q_in, halo, kx, kt, both, back, m1, l8, acc, lse, rows, att, edge,
     at_in, eb, am, ap, igs, igp, dos, do_in, mx, ge, cs, mk, cf, wg, wg_in,
     kg, k1, k2, ksum, kall, st_a, st_b, sd_a, sd_b, pt_a, pt_b, ds_a, ds_b, top, dqa, dks, dkv_in, dqs, dq_in,
-    kv_s, kv_r, q_s, q_r, h_s, h_r, a_s, a_r, e_s, e_r, d_s, d_r, p_s, p_r,
+    met, kv_s, kv_r, q_s, q_r, h_s, h_r, a_s, a_r, e_s, e_r, d_s, d_r, p_s, p_r,
     f_s, f_r, r_s, r_r, w_s, w_r, k1_s, k1_r, k2_s, k2_r, k3_s, k3_r, g_s, g_r, y_s, y_r,
 ):
     dp, me = lax.axis_index("dp"), lax.axis_index("ctx")
@@ -77,8 +77,11 @@
     def signal(where):
         pl.semaphore_signal(barrier, inc=1, device_id=where, device_id_type=MESH)
 
-    loop(1, 64, lambda d: signal(chip_at(d)))
-    loop(0, 8, lambda d: signal({"dp": (d // 4) * 2 + 1 - core, "ctx": plane * 4 + d % 4}))
+    beyond = {"dp": (dp + 2) % 4}
+    up, down = {"ctx": plane * 4 + (part + 1) % 4}, {"ctx": plane * 4 + (part + 3) % 4}
+    loop(1, 8, lambda d: signal(plane_at(d)))
+    for where in (up, down, {"ctx": (me + 1) % 32}, {"ctx": (me + 31) % 32}, partner, beyond):
+        signal(where)
 
     for c in loads[:3]:
         c.wait()
@@ -100,7 +103,7 @@
         one = lambda s: jnp.where(pos >= s, 1, 0)
         return one(s1) + one(s2) + one(s3)
 
-    pl.semaphore_wait(barrier, 71)
+    pl.semaphore_wait(barrier, 13)
 
     q_copy = lambda d: remote(qs.at[(plane + d) % 8], q_in.at[d], q_s.at[d], q_r.at[d], plane_at(d))
     slot = lambda e, f: f // 2 * 16 + 2 * e + f % 2
@@ -108,7 +111,6 @@
     kv_copy = lambda e: remote(
         kvs.at[(plane + e) % 8], kv_in.at[slot(e, 0)], kv_s.at[e], kv_r.at[e], plane_at(e)
     )
-    up, down = {"ctx": plane * 4 + (part + 1) % 4}, {"ctx": plane * 4 + (part + 3) % 4}
 
     def pass_on(e, n):
         return remote(
@@ -263,6 +265,7 @@
         spread(t + 1, st_b, pt_b, *w)
 
     loop(0, NB // 2, forward_step)
+    pl.semaphore_signal(met, inc=1, device_id=beyond, device_id_type=MESH)
     for i in range(H):
         cols = slice(i * T, (i + 1) * T)
         total = jnp.sum(l8[:, cols], axis=0, keepdims=True)
@@ -316,6 +319,7 @@
 
     am[...] = at_in[...].astype(F32).reshape(H * E, T).T.astype(BF)
     pair = lambda src, dst, n: remote(src, dst, p_s.at[n], p_r.at[n], partner)
+    pl.semaphore_wait(met, 1)
     send_att = pair(am, ap, 0)
     send_att.start()
     sides = jnp.concatenate(
@@ -566,6 +570,7 @@
             V((H, E, T), BF),
             V((H, E, T), BF),
         ]
+        + [pltpu.SemaphoreType.REGULAR]
         + [dma((n,)) for n in (8, 8, 8, 8)]
         + [dma((2, 2))] * 2
         + [dma((8,))] * 2

time: 82.2 us -> 81.6 us (level)
  no operation moved by 1% of the time
where the time goes in v8:
time: 81.6 us; the launch traced here: 81.4 us
  Pallas kernels  80.7 us (99%)
    pallas_call x1, Pallas kernels, layer(): pl.pallas_call(layer_kernel, name='layer', out_shape=(jax.ShapeDtypeStruc...  78.6 us
    pallas_call x1, Pallas kernels, hand_on(): pl.pallas_call(hand_on_kernel, name='hand_on', out_shape=tuple(shapes) +...  2.14 us

profile of v8, /device:TPU:1, one launch (start us, length us, event | category | flops | bytes accessed | tf_op | source)
XLA Modules:
  0.0 81.4 jit_solution(13229755318355638503)
XLA Ops:
  0.6 78.6 %layer.1 = (bf16[128,1024]{1,0:T(8,128)(2,1)}, bf16[128,1024]{1,0:T(8,128)(2,1)}, bf16[128,512]{1,0:T(8,128)(2,1)}, bf16[128,512]{1,0:T(8,128)(2,1)}, bf16[128,5...) custom-call(s32[4,4]{1,0:T(4,128)} %len_ref.1, bf16[128,512]{1,0:T(8,128)(2,1)} %q_hbm.1, ...), custom_call_target="tpu_custom_call" | custom-call | tf_op jit(solution)/shard_map/layer/pallas_call | solution.py:498
  79.2 2.1 %hand_on.1 = (bf16[128,1024]{1,0:T(8,128)(2,1)}, bf16[128,1024]{1,0:T(8,128)(2,1)}, bf16[128,512]{1,0:T(8,128)(2,1)}, bf16[128,512]{1,0:T(8,128)(2,1)}, bf16[128...) custom-call(bf16[128,1024]{1,0:T(8,128)(2,1)} %get-tuple-element.21.a, ...), custom_call_target="tpu_custom_call" | custom-call | tf_op jit(solution)/shard_map/hand_on/pallas_call | solution.py:594

commit v9 on v8

--- a/solution.py
+++ b/solution.py
@@ -446,14 +446,14 @@
         t = 2 * u
         product(t + 1, sd_b)
         backward_part(t, sd_a, pt_a, ds_a)
-        product(jnp.minimum(t + 2, NB - 1), sd_a)
-        backward_part(t + 1, sd_b, pt_b, ds_b)
 
         @pl.when(u > 0)
         def _():
             g_copy(2 * t).start()
 
         g_copy(2 * t + 1).start()
+        product(jnp.minimum(t + 2, NB - 1), sd_a)
+        backward_part(t + 1, sd_b, pt_b, ds_b)
         g_copy(2 * t + 2).start()
         g_copy(2 * t + 3).start()
 

time: 81.6 us -> 81.8 us (level)
  no operation moved by 1% of the time
where the time goes in v9:
time: 81.8 us; the launch traced here: 81.5 us
  Pallas kernels  80.9 us (99%)
    pallas_call x1, Pallas kernels, layer(): pl.pallas_call(layer_kernel, name='layer', out_shape=(jax.ShapeDtypeStruc...  78.8 us
    pallas_call x1, Pallas kernels, hand_on(): pl.pallas_call(hand_on_kernel, name='hand_on', out_shape=tuple(shapes) +...  2.14 us

profile of v9, /device:TPU:1, one launch (start us, length us, event | category | flops | bytes accessed | tf_op | source)
XLA Modules:
  0.0 81.5 jit_solution(3357188010542057374)
XLA Ops:
  0.6 78.8 %layer.1 = (bf16[128,1024]{1,0:T(8,128)(2,1)}, bf16[128,1024]{1,0:T(8,128)(2,1)}, bf16[128,512]{1,0:T(8,128)(2,1)}, bf16[128,512]{1,0:T(8,128)(2,1)}, bf16[128,5...) custom-call(s32[4,4]{1,0:T(4,128)} %len_ref.1, bf16[128,512]{1,0:T(8,128)(2,1)} %q_hbm.1, ...), custom_call_target="tpu_custom_call" | custom-call | tf_op jit(solution)/shard_map/layer/pallas_call | solution.py:498
  79.4 2.1 %hand_on.1 = (bf16[128,1024]{1,0:T(8,128)(2,1)}, bf16[128,1024]{1,0:T(8,128)(2,1)}, bf16[128,512]{1,0:T(8,128)(2,1)}, bf16[128,512]{1,0:T(8,128)(2,1)}, bf16[128...) custom-call(bf16[128,1024]{1,0:T(8,128)(2,1)} %get-tuple-element.21.a, ...), custom_call_target="tpu_custom_call" | custom-call | tf_op jit(solution)/shard_map/hand_on/pallas_call | solution.py:594
